TPU v7x, 512 devices: a whole 4x8x8 slice. The times are simulated.
512 devices in a mesh: space: 32 (over z, x), vel: 16 (over y, core).
Axes of the slice: x: 4, y: 8, z: 8, core: 2. Of those that a mesh axis runs over, the one named last changes fastest.
Arguments:
- distribution: float32 [128, 32, 2, 4096], P('space', None, None, 'vel'), may hold values from 0.0004 to 1, as said below
- wall_mask: int32 [128, 2, 2], P('space'), may hold values 0 or 1
- grid_point: int32 [4096], P('vel'), may hold values from 0 to 4095, as said below
- mirror_slot: int32 [4096], P('vel'), may hold values from 0 to 4095, as said below
Outputs:
- swept: float32 [128, 32, 2, 4096], P('space', None, None, 'vel')
Inputs may be any that keep to these rules, and one draw needn't show every extreme that they name: grid_point is a permutation of 0 .. 4095. mirror_slot is a permutation; slot mirror_slot[s] holds the velocity of slot s with its second component negated. `distribution`: every entry is positive.
All inputs are finite; a program needn't handle non-finite values. No bound on the sum of `wall_mask` on one device may be relied on, other than what follows from the above.
Results may differ from a plain program's by a relative error of at most 0.0003.
Values sent between devices are 32-bit elements; how exact they have to be, the bound alone decides.
No kernel may reach another device: no remote copies, remote signals or barrier semaphores. Data moves between devices by JAX's collectives and lax.ppermute only.
A program may use at most 64 MiB of HBM per device.

v0:
```python
import math

import jax
import jax.numpy as jnp
from jax import lax
from jax.sharding import PartitionSpec as P

VS = 16


stream_x = 40.0
stream_y = 0.15
stream_z = 0.05
relaxation_multiplier = 0.05
shear_power_index = 0.81
diffusivity_ratio = 2.0 / 3.0


def passed_along(x, axis, by):
    size = lax.axis_size(axis)
    pairs = [(i, i + by) for i in range(size) if 0 <= i + by < size]
    return lax.ppermute(x, axis, pairs)


def velocity_table(grid_point, side):
    spacing = 8.0 / side
    half = (side - 1) / 2.0
    first = (grid_point // (side * side)).astype(jnp.float32)
    quadratic_average = (grid_point // side % side).astype(jnp.float32)
    third = (grid_point % side).astype(jnp.float32)
    return jnp.stack(
        [(first - half) * spacing, (quadratic_average - half) * spacing, (third - half) * spacing]
    )


def velocity_sums(table, flat, integration_coefficient):
    return integration_coefficient * lax.dot_general(
        table,
        flat,
        (((1,), (1,)), ((), ())),
        precision=lax.Precision.HIGHEST,
        preferred_element_type=jnp.float32,
    )


def compose(earlier, later):
    return (later[0] * earlier[0], later[0] * earlier[1] + later[1])


def shards(distribution, wall_mask, grid_point, mirror_slot):
    integration_coefficient = (8.0 / VS) ** 3
    xi = velocity_table(grid_point, VS)
    depth, rows, planes, width = distribution.shape
    cells = depth * rows * planes
    flat = distribution.reshape(cells, width)
    wall_rows = jnp.stack([distribution[:, 0], distribution[:, rows - 1]], axis=1)
    gathered = lax.all_gather(wall_rows, "vel", axis=3, tiled=True)
    mirrored = jnp.take(gathered, mirror_slot, axis=3)
    unity = jnp.ones_like(xi[0])
    first_table = jnp.stack([unity, xi[0], xi[1], xi[2]])
    totals = lax.psum(velocity_sums(first_table, flat, integration_coefficient), "vel")
    particle_concentration = totals[0]
    flow = totals[1:] / particle_concentration[None]
    peculiar = xi[:, None, :] - flow[:, :, None]
    magnitude_square = jnp.sum(peculiar * peculiar, axis=0)
    weighted = magnitude_square * flat
    second_part = jnp.stack(
        [integration_coefficient * jnp.sum(weighted, -1)]
        + [0.5 * integration_coefficient * jnp.sum(peculiar[k] * weighted, -1) for k in range(3)]
    )
    quadratic_average = lax.psum(second_part, "vel")
    kinetic_heat_level = quadratic_average[0] / (3.0 * particle_concentration)
    heat = quadratic_average[1:]
    thermal_level_group = kinetic_heat_level[:, None]
    particle_concentration_local = particle_concentration[:, None]
    gaussian_equilibrium = (
        particle_concentration_local
        / (2.0 * math.pi * thermal_level_group) ** 1.5
        * jnp.exp(-magnitude_square / (2.0 * thermal_level_group))
    )
    lengthwise = (
        peculiar[0] * heat[0][:, None]
        + peculiar[1] * heat[1][:, None]
        + peculiar[2] * heat[2][:, None]
    )
    corrected_equilibrium = gaussian_equilibrium * (
        1.0
        + (1.0 - diffusivity_ratio)
        * lengthwise
        / (5.0 * particle_concentration_local * thermal_level_group * thermal_level_group)
        * (magnitude_square / thermal_level_group - 5.0)
    )
    relaxation_frequency = (
        relaxation_multiplier
        * particle_concentration
        * kinetic_heat_level ** (1.0 - shear_power_index)
    )
    corrected_equilibrium = corrected_equilibrium.reshape(depth, rows, planes, width)
    relaxation_frequency = relaxation_frequency.reshape(depth, rows, planes, 1)
    ghost_low = jnp.where(
        wall_mask[:, 0, :, None] == 1, mirrored[:, 0], corrected_equilibrium[:, 0]
    )
    ghost_high = jnp.where(
        wall_mask[:, 1, :, None] == 1, mirrored[:, 1], corrected_equilibrium[:, rows - 1]
    )
    padded = jnp.concatenate([ghost_low[:, None], distribution, ghost_high[:, None]], axis=1)
    below = padded[:, :-2]
    above = padded[:, 2:]
    y_flux = xi[1] * jnp.where(xi[1] > 0, distribution - below, above - distribution)
    z_flux = xi[2] * jnp.where(
        xi[2] > 0,
        distribution - jnp.roll(distribution, 1, axis=2),
        jnp.roll(distribution, -1, axis=2) - distribution,
    )
    sigma = stream_x * jnp.abs(xi[0])
    denom = 1.0 + sigma + relaxation_frequency
    coef_a = sigma / denom
    coef_b = (
        distribution
        + relaxation_frequency * corrected_equilibrium
        - stream_y * y_flux
        - stream_z * z_flux
    ) / denom
    first_block = lax.axis_index("space") == 0
    last_block = lax.axis_index("space") == lax.axis_size("space") - 1
    down_a = coef_a.at[0].set(jnp.where(first_block, 0.0, coef_a[0]))
    down_b = coef_b.at[0].set(
        jnp.where(first_block, coef_b[0] + coef_a[0] * corrected_equilibrium[0], coef_b[0])
    )
    up_a = coef_a.at[depth - 1].set(jnp.where(last_block, 0.0, coef_a[depth - 1]))
    up_b = coef_b.at[depth - 1].set(
        jnp.where(
            last_block,
            coef_b[depth - 1] + coef_a[depth - 1] * corrected_equilibrium[depth - 1],
            coef_b[depth - 1],
        )
    )
    down_a, down_b = lax.associative_scan(compose, (down_a, down_b), axis=0)
    flip_a, flip_b = lax.associative_scan(compose, (jnp.flip(up_a, 0), jnp.flip(up_b, 0)), axis=0)
    up_a = jnp.flip(flip_a, 0)
    up_b = jnp.flip(flip_b, 0)
    block_down = (down_a[depth - 1], down_b[depth - 1])
    block_up = (up_a[0], up_b[0])

    def relay_step(step, faces):
        out_down = block_down[0] * faces[0] + block_down[1]
        out_up = block_up[0] * faces[1] + block_up[1]
        return (passed_along(out_down, "space", 1), passed_along(out_up, "space", -1))

    zero_face = jnp.zeros_like(block_down[1])
    enter_down, enter_up = lax.fori_loop(
        0, lax.axis_size("space") - 1, relay_step, (zero_face, zero_face)
    )
    downstream = down_a * enter_down[None] + down_b
    upstream = up_a * enter_up[None] + up_b
    return jnp.where(xi[0] > 0, downstream, upstream)


def solution(mesh):
    placed = (P("space", None, None, "vel"), P("space", None, None), P("vel"), P("vel"))
    return jax.shard_map(
        shards, mesh=mesh, in_specs=placed, out_specs=P("space", None, None, "vel"), check_vma=False
    )
```

profile of v0, /device:TPU:198, one launch (start us, length us, event | category | flops | bytes accessed | tf_op | source)
XLA Modules:
  0.0 482.1 jit_solution(5582581152653717376)
XLA Ops:
  2.2 26.5 %psum.14 = f32[4,256]{1,0:T(4,128)S(1)} all-reduce(f32[4,256]{1,0:T(4,128)S(1)} %convolution_multiply_fusion), channel_id=1, replica_groups=mesh['space'=32,'vel'=16] {'vel'}, use_global_device_ids=true, to_apply=%region_0.1 | all-reduce | flops 1024 | bytes 8192 | tf_op jit(solution)/shard_map/psum | solution.py:61
  30.6 23.6 %psum.15 = f32[4,256]{1,0:T(4,128)S(1)} all-reduce(f32[4,256]{1,0:T(4,128)S(1)} %pad_maximum_fusion.9), channel_id=1, replica_groups=mesh['space'=32,'vel'=16] {'vel'}, use_global_device_ids=true, to_apply=%region_6.7 | all-reduce | flops 1024 | bytes 8192 | tf_op jit(solution)/shard_map/psum | solution.py:71
  57.1 56.8 %all_gather.3 = f32[4,2,2,4096]{0,2,3,1:T(2,128)} all-gather(f32[4,2,2,256]{0,2,3,1:T(2,128)S(1)} %copy.310), channel_id=1, replica_groups=mesh['space'=32,'vel'=16] {'vel'}, dimensions={3}, use_global_device_ids=true | all-gather | bytes 278528 | tf_op jit(solution)/shard_map/all_gather | solution.py:57
  121.2 359.7 %while.16 = (s32[]{:T(128)}, f32[32,2,256]{2,1,0:T(2,128)S(1)}, f32[32,2,256]{2,1,0:T(2,128)S(1)}, f32[32,2,256]{2,1,0:T(2,128)S(1)}, f32[32,2,256]{2,1,0:T(2,12...) while((s32[]{:T(128)}, f32[32,2,256]{2,1,0:T(2,128)S(1)}, ...), condition=%wide.region_8.9_spmd, body=%wide.region_7.8_spmd.sunk | while | flops 65538 | bytes 1048741 | solution.py:151
  121.3 5.4 %collective-permute-start = (f32[32,2,256]{2,1,0:T(2,128)S(1)}, f32[32,2,256]{2,1,0:T(2,128)S(1)}, u32[]{:S(2)}, u32[]{:S(2)}) collective-permute-start(f32[32,2,256]{2,1,0:T(2,128)S(1)} %bitcast.88), channel_id=1, source_target_pairs={{0,16},{16,32},{32,48},{48,64},{64,80},{80,96},{96,112},{112,128},... | collective-permute-start | bytes 196616 | tf_op jit(solution)/shard_map/while/body/eval_jaxpr/ppermute | solution.py:22
  128.6 7.5 %collective-permute-done.1 = f32[32,2,256]{2,1,0:T(2,128)S(1)} collective-permute-done((f32[32,2,256]{2,1,0:T(2,128)S(1)}, f32[32,2,256]{2,1,0:T(2,128)S(1)}, u32[]{:S(2)}, u32[]{:S(2)}) %collective-permute-start.1) | collective-permute-done | bytes 65568 | tf_op jit(solution)/shard_map/while/body/eval_jaxpr/ppermute | solution.py:22
  142.3 5.3 %collective-permute-done.1 = f32[32,2,256]{2,1,0:T(2,128)S(1)} collective-permute-done((f32[32,2,256]{2,1,0:T(2,128)S(1)}, f32[32,2,256]{2,1,0:T(2,128)S(1)}, u32[]{:S(2)}, u32[]{:S(2)}) %collective-permute-start.1) | collective-permute-done | bytes 65568 | tf_op jit(solution)/shard_map/while/body/eval_jaxpr/ppermute | solution.py:22
  153.8 5.3 %collective-permute-done.1 = f32[32,2,256]{2,1,0:T(2,128)S(1)} collective-permute-done((f32[32,2,256]{2,1,0:T(2,128)S(1)}, f32[32,2,256]{2,1,0:T(2,128)S(1)}, u32[]{:S(2)}, u32[]{:S(2)}) %collective-permute-start.1) | collective-permute-done | bytes 65568 | tf_op jit(solution)/shard_map/while/body/eval_jaxpr/ppermute | solution.py:22
  165.2 5.3 %collective-permute-done.1 = f32[32,2,256]{2,1,0:T(2,128)S(1)} collective-permute-done((f32[32,2,256]{2,1,0:T(2,128)S(1)}, f32[32,2,256]{2,1,0:T(2,128)S(1)}, u32[]{:S(2)}, u32[]{:S(2)}) %collective-permute-start.1) | collective-permute-done | bytes 65568 | tf_op jit(solution)/shard_map/while/body/eval_jaxpr/ppermute | solution.py:22
  176.7 5.3 %collective-permute-done.1 = f32[32,2,256]{2,1,0:T(2,128)S(1)} collective-permute-done((f32[32,2,256]{2,1,0:T(2,128)S(1)}, f32[32,2,256]{2,1,0:T(2,128)S(1)}, u32[]{:S(2)}, u32[]{:S(2)}) %collective-permute-start.1) | collective-permute-done | bytes 65568 | tf_op jit(solution)/shard_map/while/body/eval_jaxpr/ppermute | solution.py:22
  188.1 5.3 %collective-permute-done.1 = f32[32,2,256]{2,1,0:T(2,128)S(1)} collective-permute-done((f32[32,2,256]{2,1,0:T(2,128)S(1)}, f32[32,2,256]{2,1,0:T(2,128)S(1)}, u32[]{:S(2)}, u32[]{:S(2)}) %collective-permute-start.1) | collective-permute-done | bytes 65568 | tf_op jit(solution)/shard_map/while/body/eval_jaxpr/ppermute | solution.py:22
  199.6 5.3 %collective-permute-done.1 = f32[32,2,256]{2,1,0:T(2,128)S(1)} collective-permute-done((f32[32,2,256]{2,1,0:T(2,128)S(1)}, f32[32,2,256]{2,1,0:T(2,128)S(1)}, u32[]{:S(2)}, u32[]{:S(2)}) %collective-permute-start.1) | collective-permute-done | bytes 65568 | tf_op jit(solution)/shard_map/while/body/eval_jaxpr/ppermute | solution.py:22
  211.0 5.3 %collective-permute-done.1 = f32[32,2,256]{2,1,0:T(2,128)S(1)} collective-permute-done((f32[32,2,256]{2,1,0:T(2,128)S(1)}, f32[32,2,256]{2,1,0:T(2,128)S(1)}, u32[]{:S(2)}, u32[]{:S(2)}) %collective-permute-start.1) | collective-permute-done | bytes 65568 | tf_op jit(solution)/shard_map/while/body/eval_jaxpr/ppermute | solution.py:22
  222.9 5.3 %collective-permute-done.1 = f32[32,2,256]{2,1,0:T(2,128)S(1)} collective-permute-done((f32[32,2,256]{2,1,0:T(2,128)S(1)}, f32[32,2,256]{2,1,0:T(2,128)S(1)}, u32[]{:S(2)}, u32[]{:S(2)}) %collective-permute-start.1) | collective-permute-done | bytes 65568 | tf_op jit(solution)/shard_map/while/body/eval_jaxpr/ppermute | solution.py:22
  234.4 5.3 %collective-permute-done.1 = f32[32,2,256]{2,1,0:T(2,128)S(1)} collective-permute-done((f32[32,2,256]{2,1,0:T(2,128)S(1)}, f32[32,2,256]{2,1,0:T(2,128)S(1)}, u32[]{:S(2)}, u32[]{:S(2)}) %collective-permute-start.1) | collective-permute-done | bytes 65568 | tf_op jit(solution)/shard_map/while/body/eval_jaxpr/ppermute | solution.py:22
  245.8 5.3 %collective-permute-done.1 = f32[32,2,256]{2,1,0:T(2,128)S(1)} collective-permute-done((f32[32,2,256]{2,1,0:T(2,128)S(1)}, f32[32,2,256]{2,1,0:T(2,128)S(1)}, u32[]{:S(2)}, u32[]{:S(2)}) %collective-permute-start.1) | collective-permute-done | bytes 65568 | tf_op jit(solution)/shard_map/while/body/eval_jaxpr/ppermute | solution.py:22
  257.3 5.3 %collective-permute-done.1 = f32[32,2,256]{2,1,0:T(2,128)S(1)} collective-permute-done((f32[32,2,256]{2,1,0:T(2,128)S(1)}, f32[32,2,256]{2,1,0:T(2,128)S(1)}, u32[]{:S(2)}, u32[]{:S(2)}) %collective-permute-start.1) | collective-permute-done | bytes 65568 | tf_op jit(solution)/shard_map/while/body/eval_jaxpr/ppermute | solution.py:22
  268.7 5.3 %collective-permute-done.1 = f32[32,2,256]{2,1,0:T(2,128)S(1)} collective-permute-done((f32[32,2,256]{2,1,0:T(2,128)S(1)}, f32[32,2,256]{2,1,0:T(2,128)S(1)}, u32[]{:S(2)}, u32[]{:S(2)}) %collective-permute-start.1) | collective-permute-done | bytes 65568 | tf_op jit(solution)/shard_map/while/body/eval_jaxpr/ppermute | solution.py:22
  280.2 5.3 %collective-permute-done.1 = f32[32,2,256]{2,1,0:T(2,128)S(1)} collective-permute-done((f32[32,2,256]{2,1,0:T(2,128)S(1)}, f32[32,2,256]{2,1,0:T(2,128)S(1)}, u32[]{:S(2)}, u32[]{:S(2)}) %collective-permute-start.1) | collective-permute-done | bytes 65568 | tf_op jit(solution)/shard_map/while/body/eval_jaxpr/ppermute | solution.py:22
  291.6 5.3 %collective-permute-done.1 = f32[32,2,256]{2,1,0:T(2,128)S(1)} collective-permute-done((f32[32,2,256]{2,1,0:T(2,128)S(1)}, f32[32,2,256]{2,1,0:T(2,128)S(1)}, u32[]{:S(2)}, u32[]{:S(2)}) %collective-permute-start.1) | collective-permute-done | bytes 65568 | tf_op jit(solution)/shard_map/while/body/eval_jaxpr/ppermute | solution.py:22
  303.1 5.3 %collective-permute-done.1 = f32[32,2,256]{2,1,0:T(2,128)S(1)} collective-permute-done((f32[32,2,256]{2,1,0:T(2,128)S(1)}, f32[32,2,256]{2,1,0:T(2,128)S(1)}, u32[]{:S(2)}, u32[]{:S(2)}) %collective-permute-start.1) | collective-permute-done | bytes 65568 | tf_op jit(solution)/shard_map/while/body/eval_jaxpr/ppermute | solution.py:22
  314.5 5.3 %collective-permute-done.1 = f32[32,2,256]{2,1,0:T(2,128)S(1)} collective-permute-done((f32[32,2,256]{2,1,0:T(2,128)S(1)}, f32[32,2,256]{2,1,0:T(2,128)S(1)}, u32[]{:S(2)}, u32[]{:S(2)}) %collective-permute-start.1) | collective-permute-done | bytes 65568 | tf_op jit(solution)/shard_map/while/body/eval_jaxpr/ppermute | solution.py:22
  326.4 5.3 %collective-permute-done.1 = f32[32,2,256]{2,1,0:T(2,128)S(1)} collective-permute-done((f32[32,2,256]{2,1,0:T(2,128)S(1)}, f32[32,2,256]{2,1,0:T(2,128)S(1)}, u32[]{:S(2)}, u32[]{:S(2)}) %collective-permute-start.1) | collective-permute-done | bytes 65568 | tf_op jit(solution)/shard_map/while/body/eval_jaxpr/ppermute | solution.py:22
  337.9 5.3 %collective-permute-done.1 = f32[32,2,256]{2,1,0:T(2,128)S(1)} collective-permute-done((f32[32,2,256]{2,1,0:T(2,128)S(1)}, f32[32,2,256]{2,1,0:T(2,128)S(1)}, u32[]{:S(2)}, u32[]{:S(2)}) %collective-permute-start.1) | collective-permute-done | bytes 65568 | tf_op jit(solution)/shard_map/while/body/eval_jaxpr/ppermute | solution.py:22
  349.3 5.3 %collective-permute-done.1 = f32[32,2,256]{2,1,0:T(2,128)S(1)} collective-permute-done((f32[32,2,256]{2,1,0:T(2,128)S(1)}, f32[32,2,256]{2,1,0:T(2,128)S(1)}, u32[]{:S(2)}, u32[]{:S(2)}) %collective-permute-start.1) | collective-permute-done | bytes 65568 | tf_op jit(solution)/shard_map/while/body/eval_jaxpr/ppermute | solution.py:22
  360.8 5.3 %collective-permute-done.1 = f32[32,2,256]{2,1,0:T(2,128)S(1)} collective-permute-done((f32[32,2,256]{2,1,0:T(2,128)S(1)}, f32[32,2,256]{2,1,0:T(2,128)S(1)}, u32[]{:S(2)}, u32[]{:S(2)}) %collective-permute-start.1) | collective-permute-done | bytes 65568 | tf_op jit(solution)/shard_map/while/body/eval_jaxpr/ppermute | solution.py:22
  372.2 5.3 %collective-permute-done.1 = f32[32,2,256]{2,1,0:T(2,128)S(1)} collective-permute-done((f32[32,2,256]{2,1,0:T(2,128)S(1)}, f32[32,2,256]{2,1,0:T(2,128)S(1)}, u32[]{:S(2)}, u32[]{:S(2)}) %collective-permute-start.1) | collective-permute-done | bytes 65568 | tf_op jit(solution)/shard_map/while/body/eval_jaxpr/ppermute | solution.py:22
  383.7 5.3 %collective-permute-done.1 = f32[32,2,256]{2,1,0:T(2,128)S(1)} collective-permute-done((f32[32,2,256]{2,1,0:T(2,128)S(1)}, f32[32,2,256]{2,1,0:T(2,128)S(1)}, u32[]{:S(2)}, u32[]{:S(2)}) %collective-permute-start.1) | collective-permute-done | bytes 65568 | tf_op jit(solution)/shard_map/while/body/eval_jaxpr/ppermute | solution.py:22
  395.1 5.3 %collective-permute-done.1 = f32[32,2,256]{2,1,0:T(2,128)S(1)} collective-permute-done((f32[32,2,256]{2,1,0:T(2,128)S(1)}, f32[32,2,256]{2,1,0:T(2,128)S(1)}, u32[]{:S(2)}, u32[]{:S(2)}) %collective-permute-start.1) | collective-permute-done | bytes 65568 | tf_op jit(solution)/shard_map/while/body/eval_jaxpr/ppermute | solution.py:22
  406.6 5.3 %collective-permute-done.1 = f32[32,2,256]{2,1,0:T(2,128)S(1)} collective-permute-done((f32[32,2,256]{2,1,0:T(2,128)S(1)}, f32[32,2,256]{2,1,0:T(2,128)S(1)}, u32[]{:S(2)}, u32[]{:S(2)}) %collective-permute-start.1) | collective-permute-done | bytes 65568 | tf_op jit(solution)/shard_map/while/body/eval_jaxpr/ppermute | solution.py:22
  418.0 5.3 %collective-permute-done.1 = f32[32,2,256]{2,1,0:T(2,128)S(1)} collective-permute-done((f32[32,2,256]{2,1,0:T(2,128)S(1)}, f32[32,2,256]{2,1,0:T(2,128)S(1)}, u32[]{:S(2)}, u32[]{:S(2)}) %collective-permute-start.1) | collective-permute-done | bytes 65568 | tf_op jit(solution)/shard_map/while/body/eval_jaxpr/ppermute | solution.py:22
  429.9 5.3 %collective-permute-done.1 = f32[32,2,256]{2,1,0:T(2,128)S(1)} collective-permute-done((f32[32,2,256]{2,1,0:T(2,128)S(1)}, f32[32,2,256]{2,1,0:T(2,128)S(1)}, u32[]{:S(2)}, u32[]{:S(2)}) %collective-permute-start.1) | collective-permute-done | bytes 65568 | tf_op jit(solution)/shard_map/while/body/eval_jaxpr/ppermute | solution.py:22
  (272 shorter events, 223.6 us)
Async XLA Ops:
  121.3 7.4 %collective-permute-start = (f32[32,2,256]{2,1,0:T(2,128)S(1)}, f32[32,2,256]{2,1,0:T(2,128)S(1)}, u32[]{:S(2)}, u32[]{:S(2)}) collective-permute-start(f32[32,2,256]{2,1,0:T(2,128)S(1)} %bitcast.88), channel_id=1, source_target_pairs={{0,16},{16,32},{32,48},{48,64},{64,80},{80,96},{96,112},{112,128},... | collective-permute-start | bytes 196616 | tf_op jit(solution)/shard_map/while/body/eval_jaxpr/ppermute | solution.py:22
  126.7 9.5 %collective-permute-start.1 = (f32[32,2,256]{2,1,0:T(2,128)S(1)}, f32[32,2,256]{2,1,0:T(2,128)S(1)}, u32[]{:S(2)}, u32[]{:S(2)}) collective-permute-start(f32[32,2,256]{2,1,0:T(2,128)S(1)} %bitcast.89), channel_id=1, source_target_pairs={{16,0},{32,16},{48,32},{64,48},{80,64},{96,80},{112,96},{128,112},... | collective-permute-start | bytes 196616 | tf_op jit(solution)/shard_map/while/body/eval_jaxpr/ppermute | solution.py:22
  138.1 9.5 %collective-permute-start.1 = (f32[32,2,256]{2,1,0:T(2,128)S(1)}, f32[32,2,256]{2,1,0:T(2,128)S(1)}, u32[]{:S(2)}, u32[]{:S(2)}) collective-permute-start(f32[32,2,256]{2,1,0:T(2,128)S(1)} %bitcast.89), channel_id=1, source_target_pairs={{16,0},{32,16},{48,32},{64,48},{80,64},{96,80},{112,96},{128,112},... | collective-permute-start | bytes 196616 | tf_op jit(solution)/shard_map/while/body/eval_jaxpr/ppermute | solution.py:22
  149.6 9.5 %collective-permute-start.1 = (f32[32,2,256]{2,1,0:T(2,128)S(1)}, f32[32,2,256]{2,1,0:T(2,128)S(1)}, u32[]{:S(2)}, u32[]{:S(2)}) collective-permute-start(f32[32,2,256]{2,1,0:T(2,128)S(1)} %bitcast.89), channel_id=1, source_target_pairs={{16,0},{32,16},{48,32},{64,48},{80,64},{96,80},{112,96},{128,112},... | collective-permute-start | bytes 196616 | tf_op jit(solution)/shard_map/while/body/eval_jaxpr/ppermute | solution.py:22
  161.0 9.5 %collective-permute-start.1 = (f32[32,2,256]{2,1,0:T(2,128)S(1)}, f32[32,2,256]{2,1,0:T(2,128)S(1)}, u32[]{:S(2)}, u32[]{:S(2)}) collective-permute-start(f32[32,2,256]{2,1,0:T(2,128)S(1)} %bitcast.89), channel_id=1, source_target_pairs={{16,0},{32,16},{48,32},{64,48},{80,64},{96,80},{112,96},{128,112},... | collective-permute-start | bytes 196616 | tf_op jit(solution)/shard_map/while/body/eval_jaxpr/ppermute | solution.py:22
  172.5 9.5 %collective-permute-start.1 = (f32[32,2,256]{2,1,0:T(2,128)S(1)}, f32[32,2,256]{2,1,0:T(2,128)S(1)}, u32[]{:S(2)}, u32[]{:S(2)}) collective-permute-start(f32[32,2,256]{2,1,0:T(2,128)S(1)} %bitcast.89), channel_id=1, source_target_pairs={{16,0},{32,16},{48,32},{64,48},{80,64},{96,80},{112,96},{128,112},... | collective-permute-start | bytes 196616 | tf_op jit(solution)/shard_map/while/body/eval_jaxpr/ppermute | solution.py:22
  183.9 9.5 %collective-permute-start.1 = (f32[32,2,256]{2,1,0:T(2,128)S(1)}, f32[32,2,256]{2,1,0:T(2,128)S(1)}, u32[]{:S(2)}, u32[]{:S(2)}) collective-permute-start(f32[32,2,256]{2,1,0:T(2,128)S(1)} %bitcast.89), channel_id=1, source_target_pairs={{16,0},{32,16},{48,32},{64,48},{80,64},{96,80},{112,96},{128,112},... | collective-permute-start | bytes 196616 | tf_op jit(solution)/shard_map/while/body/eval_jaxpr/ppermute | solution.py:22
  195.4 9.5 %collective-permute-start.1 = (f32[32,2,256]{2,1,0:T(2,128)S(1)}, f32[32,2,256]{2,1,0:T(2,128)S(1)}, u32[]{:S(2)}, u32[]{:S(2)}) collective-permute-start(f32[32,2,256]{2,1,0:T(2,128)S(1)} %bitcast.89), channel_id=1, source_target_pairs={{16,0},{32,16},{48,32},{64,48},{80,64},{96,80},{112,96},{128,112},... | collective-permute-start | bytes 196616 | tf_op jit(solution)/shard_map/while/body/eval_jaxpr/ppermute | solution.py:22
  206.8 9.5 %collective-permute-start.1 = (f32[32,2,256]{2,1,0:T(2,128)S(1)}, f32[32,2,256]{2,1,0:T(2,128)S(1)}, u32[]{:S(2)}, u32[]{:S(2)}) collective-permute-start(f32[32,2,256]{2,1,0:T(2,128)S(1)} %bitcast.89), channel_id=1, source_target_pairs={{16,0},{32,16},{48,32},{64,48},{80,64},{96,80},{112,96},{128,112},... | collective-permute-start | bytes 196616 | tf_op jit(solution)/shard_map/while/body/eval_jaxpr/ppermute | solution.py:22
  218.3 10.0 %collective-permute-start.1 = (f32[32,2,256]{2,1,0:T(2,128)S(1)}, f32[32,2,256]{2,1,0:T(2,128)S(1)}, u32[]{:S(2)}, u32[]{:S(2)}) collective-permute-start(f32[32,2,256]{2,1,0:T(2,128)S(1)} %bitcast.89), channel_id=1, source_target_pairs={{16,0},{32,16},{48,32},{64,48},{80,64},{96,80},{112,96},{128,112},... | collective-permute-start | bytes 196616 | tf_op jit(solution)/shard_map/while/body/eval_jaxpr/ppermute | solution.py:22
  230.2 9.5 %collective-permute-start.1 = (f32[32,2,256]{2,1,0:T(2,128)S(1)}, f32[32,2,256]{2,1,0:T(2,128)S(1)}, u32[]{:S(2)}, u32[]{:S(2)}) collective-permute-start(f32[32,2,256]{2,1,0:T(2,128)S(1)} %bitcast.89), channel_id=1, source_target_pairs={{16,0},{32,16},{48,32},{64,48},{80,64},{96,80},{112,96},{128,112},... | collective-permute-start | bytes 196616 | tf_op jit(solution)/shard_map/while/body/eval_jaxpr/ppermute | solution.py:22
  241.6 9.5 %collective-permute-start.1 = (f32[32,2,256]{2,1,0:T(2,128)S(1)}, f32[32,2,256]{2,1,0:T(2,128)S(1)}, u32[]{:S(2)}, u32[]{:S(2)}) collective-permute-start(f32[32,2,256]{2,1,0:T(2,128)S(1)} %bitcast.89), channel_id=1, source_target_pairs={{16,0},{32,16},{48,32},{64,48},{80,64},{96,80},{112,96},{128,112},... | collective-permute-start | bytes 196616 | tf_op jit(solution)/shard_map/while/body/eval_jaxpr/ppermute | solution.py:22
  253.1 9.5 %collective-permute-start.1 = (f32[32,2,256]{2,1,0:T(2,128)S(1)}, f32[32,2,256]{2,1,0:T(2,128)S(1)}, u32[]{:S(2)}, u32[]{:S(2)}) collective-permute-start(f32[32,2,256]{2,1,0:T(2,128)S(1)} %bitcast.89), channel_id=1, source_target_pairs={{16,0},{32,16},{48,32},{64,48},{80,64},{96,80},{112,96},{128,112},... | collective-permute-start | bytes 196616 | tf_op jit(solution)/shard_map/while/body/eval_jaxpr/ppermute | solution.py:22
  264.5 9.5 %collective-permute-start.1 = (f32[32,2,256]{2,1,0:T(2,128)S(1)}, f32[32,2,256]{2,1,0:T(2,128)S(1)}, u32[]{:S(2)}, u32[]{:S(2)}) collective-permute-start(f32[32,2,256]{2,1,0:T(2,128)S(1)} %bitcast.89), channel_id=1, source_target_pairs={{16,0},{32,16},{48,32},{64,48},{80,64},{96,80},{112,96},{128,112},... | collective-permute-start | bytes 196616 | tf_op jit(solution)/shard_map/while/body/eval_jaxpr/ppermute | solution.py:22
  276.0 9.5 %collective-permute-start.1 = (f32[32,2,256]{2,1,0:T(2,128)S(1)}, f32[32,2,256]{2,1,0:T(2,128)S(1)}, u32[]{:S(2)}, u32[]{:S(2)}) collective-permute-start(f32[32,2,256]{2,1,0:T(2,128)S(1)} %bitcast.89), channel_id=1, source_target_pairs={{16,0},{32,16},{48,32},{64,48},{80,64},{96,80},{112,96},{128,112},... | collective-permute-start | bytes 196616 | tf_op jit(solution)/shard_map/while/body/eval_jaxpr/ppermute | solution.py:22
  287.4 9.5 %collective-permute-start.1 = (f32[32,2,256]{2,1,0:T(2,128)S(1)}, f32[32,2,256]{2,1,0:T(2,128)S(1)}, u32[]{:S(2)}, u32[]{:S(2)}) collective-permute-start(f32[32,2,256]{2,1,0:T(2,128)S(1)} %bitcast.89), channel_id=1, source_target_pairs={{16,0},{32,16},{48,32},{64,48},{80,64},{96,80},{112,96},{128,112},... | collective-permute-start | bytes 196616 | tf_op jit(solution)/shard_map/while/body/eval_jaxpr/ppermute | solution.py:22
  298.9 9.5 %collective-permute-start.1 = (f32[32,2,256]{2,1,0:T(2,128)S(1)}, f32[32,2,256]{2,1,0:T(2,128)S(1)}, u32[]{:S(2)}, u32[]{:S(2)}) collective-permute-start(f32[32,2,256]{2,1,0:T(2,128)S(1)} %bitcast.89), channel_id=1, source_target_pairs={{16,0},{32,16},{48,32},{64,48},{80,64},{96,80},{112,96},{128,112},... | collective-permute-start | bytes 196616 | tf_op jit(solution)/shard_map/while/body/eval_jaxpr/ppermute | solution.py:22
  310.3 9.5 %collective-permute-start.1 = (f32[32,2,256]{2,1,0:T(2,128)S(1)}, f32[32,2,256]{2,1,0:T(2,128)S(1)}, u32[]{:S(2)}, u32[]{:S(2)}) collective-permute-start(f32[32,2,256]{2,1,0:T(2,128)S(1)} %bitcast.89), channel_id=1, source_target_pairs={{16,0},{32,16},{48,32},{64,48},{80,64},{96,80},{112,96},{128,112},... | collective-permute-start | bytes 196616 | tf_op jit(solution)/shard_map/while/body/eval_jaxpr/ppermute | solution.py:22
  321.8 9.9 %collective-permute-start.1 = (f32[32,2,256]{2,1,0:T(2,128)S(1)}, f32[32,2,256]{2,1,0:T(2,128)S(1)}, u32[]{:S(2)}, u32[]{:S(2)}) collective-permute-start(f32[32,2,256]{2,1,0:T(2,128)S(1)} %bitcast.89), channel_id=1, source_target_pairs={{16,0},{32,16},{48,32},{64,48},{80,64},{96,80},{112,96},{128,112},... | collective-permute-start | bytes 196616 | tf_op jit(solution)/shard_map/while/body/eval_jaxpr/ppermute | solution.py:22
  333.7 9.5 %collective-permute-start.1 = (f32[32,2,256]{2,1,0:T(2,128)S(1)}, f32[32,2,256]{2,1,0:T(2,128)S(1)}, u32[]{:S(2)}, u32[]{:S(2)}) collective-permute-start(f32[32,2,256]{2,1,0:T(2,128)S(1)} %bitcast.89), channel_id=1, source_target_pairs={{16,0},{32,16},{48,32},{64,48},{80,64},{96,80},{112,96},{128,112},... | collective-permute-start | bytes 196616 | tf_op jit(solution)/shard_map/while/body/eval_jaxpr/ppermute | solution.py:22
  345.1 9.5 %collective-permute-start.1 = (f32[32,2,256]{2,1,0:T(2,128)S(1)}, f32[32,2,256]{2,1,0:T(2,128)S(1)}, u32[]{:S(2)}, u32[]{:S(2)}) collective-permute-start(f32[32,2,256]{2,1,0:T(2,128)S(1)} %bitcast.89), channel_id=1, source_target_pairs={{16,0},{32,16},{48,32},{64,48},{80,64},{96,80},{112,96},{128,112},... | collective-permute-start | bytes 196616 | tf_op jit(solution)/shard_map/while/body/eval_jaxpr/ppermute | solution.py:22
  356.6 9.5 %collective-permute-start.1 = (f32[32,2,256]{2,1,0:T(2,128)S(1)}, f32[32,2,256]{2,1,0:T(2,128)S(1)}, u32[]{:S(2)}, u32[]{:S(2)}) collective-permute-start(f32[32,2,256]{2,1,0:T(2,128)S(1)} %bitcast.89), channel_id=1, source_target_pairs={{16,0},{32,16},{48,32},{64,48},{80,64},{96,80},{112,96},{128,112},... | collective-permute-start | bytes 196616 | tf_op jit(solution)/shard_map/while/body/eval_jaxpr/ppermute | solution.py:22
  368.0 9.5 %collective-permute-start.1 = (f32[32,2,256]{2,1,0:T(2,128)S(1)}, f32[32,2,256]{2,1,0:T(2,128)S(1)}, u32[]{:S(2)}, u32[]{:S(2)}) collective-permute-start(f32[32,2,256]{2,1,0:T(2,128)S(1)} %bitcast.89), channel_id=1, source_target_pairs={{16,0},{32,16},{48,32},{64,48},{80,64},{96,80},{112,96},{128,112},... | collective-permute-start | bytes 196616 | tf_op jit(solution)/shard_map/while/body/eval_jaxpr/ppermute | solution.py:22
  379.4 9.5 %collective-permute-start.1 = (f32[32,2,256]{2,1,0:T(2,128)S(1)}, f32[32,2,256]{2,1,0:T(2,128)S(1)}, u32[]{:S(2)}, u32[]{:S(2)}) collective-permute-start(f32[32,2,256]{2,1,0:T(2,128)S(1)} %bitcast.89), channel_id=1, source_target_pairs={{16,0},{32,16},{48,32},{64,48},{80,64},{96,80},{112,96},{128,112},... | collective-permute-start | bytes 196616 | tf_op jit(solution)/shard_map/while/body/eval_jaxpr/ppermute | solution.py:22
  390.9 9.5 %collective-permute-start.1 = (f32[32,2,256]{2,1,0:T(2,128)S(1)}, f32[32,2,256]{2,1,0:T(2,128)S(1)}, u32[]{:S(2)}, u32[]{:S(2)}) collective-permute-start(f32[32,2,256]{2,1,0:T(2,128)S(1)} %bitcast.89), channel_id=1, source_target_pairs={{16,0},{32,16},{48,32},{64,48},{80,64},{96,80},{112,96},{128,112},... | collective-permute-start | bytes 196616 | tf_op jit(solution)/shard_map/while/body/eval_jaxpr/ppermute | solution.py:22
  402.3 9.5 %collective-permute-start.1 = (f32[32,2,256]{2,1,0:T(2,128)S(1)}, f32[32,2,256]{2,1,0:T(2,128)S(1)}, u32[]{:S(2)}, u32[]{:S(2)}) collective-permute-start(f32[32,2,256]{2,1,0:T(2,128)S(1)} %bitcast.89), channel_id=1, source_target_pairs={{16,0},{32,16},{48,32},{64,48},{80,64},{96,80},{112,96},{128,112},... | collective-permute-start | bytes 196616 | tf_op jit(solution)/shard_map/while/body/eval_jaxpr/ppermute | solution.py:22
  413.8 9.5 %collective-permute-start.1 = (f32[32,2,256]{2,1,0:T(2,128)S(1)}, f32[32,2,256]{2,1,0:T(2,128)S(1)}, u32[]{:S(2)}, u32[]{:S(2)}) collective-permute-start(f32[32,2,256]{2,1,0:T(2,128)S(1)} %bitcast.89), channel_id=1, source_target_pairs={{16,0},{32,16},{48,32},{64,48},{80,64},{96,80},{112,96},{128,112},... | collective-permute-start | bytes 196616 | tf_op jit(solution)/shard_map/while/body/eval_jaxpr/ppermute | solution.py:22
  425.2 9.9 %collective-permute-start.1 = (f32[32,2,256]{2,1,0:T(2,128)S(1)}, f32[32,2,256]{2,1,0:T(2,128)S(1)}, u32[]{:S(2)}, u32[]{:S(2)}) collective-permute-start(f32[32,2,256]{2,1,0:T(2,128)S(1)} %bitcast.89), channel_id=1, source_target_pairs={{16,0},{32,16},{48,32},{64,48},{80,64},{96,80},{112,96},{128,112},... | collective-permute-start | bytes 196616 | tf_op jit(solution)/shard_map/while/body/eval_jaxpr/ppermute | solution.py:22
  437.1 9.5 %collective-permute-start.1 = (f32[32,2,256]{2,1,0:T(2,128)S(1)}, f32[32,2,256]{2,1,0:T(2,128)S(1)}, u32[]{:S(2)}, u32[]{:S(2)}) collective-permute-start(f32[32,2,256]{2,1,0:T(2,128)S(1)} %bitcast.89), channel_id=1, source_target_pairs={{16,0},{32,16},{48,32},{64,48},{80,64},{96,80},{112,96},{128,112},... | collective-permute-start | bytes 196616 | tf_op jit(solution)/shard_map/while/body/eval_jaxpr/ppermute | solution.py:22
  448.6 9.5 %collective-permute-start.1 = (f32[32,2,256]{2,1,0:T(2,128)S(1)}, f32[32,2,256]{2,1,0:T(2,128)S(1)}, u32[]{:S(2)}, u32[]{:S(2)}) collective-permute-start(f32[32,2,256]{2,1,0:T(2,128)S(1)} %bitcast.89), channel_id=1, source_target_pairs={{16,0},{32,16},{48,32},{64,48},{80,64},{96,80},{112,96},{128,112},... | collective-permute-start | bytes 196616 | tf_op jit(solution)/shard_map/while/body/eval_jaxpr/ppermute | solution.py:22
  460.0 9.5 %collective-permute-start.1 = (f32[32,2,256]{2,1,0:T(2,128)S(1)}, f32[32,2,256]{2,1,0:T(2,128)S(1)}, u32[]{:S(2)}, u32[]{:S(2)}) collective-permute-start(f32[32,2,256]{2,1,0:T(2,128)S(1)} %bitcast.89), channel_id=1, source_target_pairs={{16,0},{32,16},{48,32},{64,48},{80,64},{96,80},{112,96},{128,112},... | collective-permute-start | bytes 196616 | tf_op jit(solution)/shard_map/while/body/eval_jaxpr/ppermute | solution.py:22
  471.5 9.5 %collective-permute-start.1 = (f32[32,2,256]{2,1,0:T(2,128)S(1)}, f32[32,2,256]{2,1,0:T(2,128)S(1)}, u32[]{:S(2)}, u32[]{:S(2)}) collective-permute-start(f32[32,2,256]{2,1,0:T(2,128)S(1)} %bitcast.89), channel_id=1, source_target_pairs={{16,0},{32,16},{48,32},{64,48},{80,64},{96,80},{112,96},{128,112},... | collective-permute-start | bytes 196616 | tf_op jit(solution)/shard_map/while/body/eval_jaxpr/ppermute | solution.py:22
  (33 other events, 391.3 us)
where the time goes:
time: 486 us; the launch traced here: 482 us
  starting transfers between devices  183 us (38%)
  waiting for transfers between devices  175 us (36%)
  blocking collectives  107 us (22%)
  local copies, waits for them, and re-layouts  10.5 us (2%)
  other arithmetic  4.87 us (1%)
    ppermute x62, starting transfers between devices, passed_along(): return lax.ppermute(x, axis, pairs)  183 us
    ppermute x62, waiting for transfers between devices, passed_along(): return lax.ppermute(x, axis, pairs)  175 us
    all_gather x1, blocking collectives, shards(): gathered = lax.all_gather(wall_rows, 'vel', axis=3, tiled=True)  56.8 us
    psum x1, blocking collectives, shards(): lax.psum(velocity_sums(first_table, flat, integration_coefficient), 'vel')  26.5 us
    psum x1, blocking collectives, shards(): quadratic_average = lax.psum(second_part, 'vel')  23.6 us
  transfers between devices with their start and end apart: 62, of which 61 were waited for; matrix products, arithmetic and copies ran while one was open for 0% of the time, Pallas kernels for 0%

commit v1 on v0

v1 whole, which is shorter than its diff:
```python
import math

import jax
import jax.numpy as jnp
from jax import lax
from jax.experimental import pallas as pl
from jax.experimental.pallas import tpu as pltpu
from jax.sharding import PartitionSpec as P

VS = 16
SPACING = 8.0 / VS
HALF = (VS - 1) / 2.0
WEIGHT = SPACING**3

stream_x = 40.0
stream_y = 0.15
stream_z = 0.05
relaxation_multiplier = 0.05
shear_power_index = 0.81
diffusivity_ratio = 2.0 / 3.0

DEPTH, ROWS, PLANES, WIDTH = 4, 32, 2, 256
LANES = 128
XROWS = ROWS * 2 * PLANES
F32 = jnp.float32


def velocity(points):
    first = (points >> 8).astype(F32)
    second = ((points >> 4) & 15).astype(F32)
    third = (points & 15).astype(F32)
    return [(v - HALF) * SPACING for v in (first, second, third)]


def sublane(shape):
    return lax.broadcasted_iota(jnp.int32, shape, 0)


def by_half(pair):
    low = jnp.broadcast_to(pair[0:1], (8, LANES))
    high = jnp.broadcast_to(pair[1:2], (8, LANES))
    return jnp.where((sublane((8, LANES)) & 2) == 0, low, high)


def moments_kernel(f_ref, point_ref, out_ref):
    points = point_ref[...]
    tables = []
    for half in range(2):
        x1, x2, x3 = velocity(points[half : half + 1])
        square = x1 * x1 + x2 * x2 + x3 * x3
        zero = jnp.zeros_like(x1)
        tables += [
            jnp.ones_like(x1), x1, x2, x3,
            x1 * x1, x2 * x2, x3 * x3, x1 * x2,
            x1 * x3, x2 * x3, x1 * square, x2 * square,
            x3 * square, zero, zero, zero,
        ]
    table = jnp.concatenate(tables, axis=0)
    low_lane = (lax.broadcasted_iota(jnp.int32, (8, LANES), 1) & 2) == 0
    x2 = velocity(points)[1]
    for x in range(DEPTH):
        sums = lax.dot_general(
            table,
            f_ref[pl.ds(x * XROWS, XROWS), :],
            (((1,), (1,)), ((), ())),
            precision=lax.Precision.HIGHEST,
            preferred_element_type=F32,
        )
        packed = jnp.where(
            low_lane,
            sums[0:8] + pltpu.roll(sums[16:24], LANES - 2, 1),
            sums[24:32] + pltpu.roll(sums[8:16], 2, 1),
        )
        out_ref[pl.ds(x, 8, stride=DEPTH), :] = packed
        for half in range(2):
            low = f_ref[pl.ds(x * XROWS + 2 * half, 2), :]
            high = f_ref[pl.ds((x + 1) * XROWS - 4 + 2 * half, 2), :]
            out_ref[pl.ds(32 + 8 * half + 2 * x, 2), :] = jnp.where(
                x2[half : half + 1] < 0, low, high
            )


def cell_quantities(sums):
    low_lane = (lax.broadcasted_iota(jnp.int32, (DEPTH, LANES), 1) & 2) == 0
    low, high = [], []
    for m in range(8):
        own = sums[DEPTH * m : DEPTH * (m + 1)] * WEIGHT
        other = jnp.where(low_lane, pltpu.roll(own, LANES - 2, 1), pltpu.roll(own, 2, 1))
        low.append(jnp.where(low_lane, own, other))
        high.append(jnp.where(low_lane, other, own))
    n = low[0]
    inv = 1.0 / n
    u = [low[1 + k] * inv for k in range(3)]
    pressure = {(0, 0): low[4], (1, 1): low[5], (2, 2): low[6]}
    pressure.update({(0, 1): low[7], (0, 2): high[0], (1, 2): high[1]})
    energy = low[4] + low[5] + low[6]
    speed = u[0] * u[0] + u[1] * u[1] + u[2] * u[2]
    temperature = (energy - n * speed) * inv * (1.0 / 3.0)
    heat = []
    for k in range(3):
        cross = sum(u[j] * pressure[min(j, k), max(j, k)] for j in range(3))
        heat.append(0.5 * (high[2 + k] - 2.0 * cross + u[k] * (2.0 * n * speed - energy)))
    inv_t = 1.0 / temperature
    scale = (1.0 - diffusivity_ratio) / 5.0 * inv * inv_t * inv_t
    arg = 2.0 * math.pi * temperature
    norm = n / (arg * jnp.sqrt(arg))
    rate = relaxation_multiplier * n * jnp.exp((1.0 - shear_power_index) * jnp.log(temperature))
    return u + [h * scale for h in heat] + [inv_t, norm, rate]


def blocks_kernel(
    ends_ref, wall_ref, got_ref, f_ref, point_ref, mirror_ref, send_ref, a_ref, h_ref
):
    sums = got_ref[0, 0:32, :]
    for k in range(1, 16):
        sums = sums + got_ref[k, 0:32, :]
    quantities = cell_quantities(sums)
    filler = jnp.zeros((LANES - DEPTH * len(quantities), LANES), F32)
    columns = jnp.concatenate(quantities + [filler], axis=0).T

    mirror = mirror_ref[...]
    found = []
    for half in range(2):
        slot = jnp.broadcast_to(mirror[half : half + 1], (8, LANES))
        lane, group = slot & (LANES - 1), slot >> 7
        value = jnp.zeros((8, LANES), F32)
        for source in range(32):
            piece = got_ref[source // 2, pl.ds(32 + 8 * (source % 2), 8), :]
            value = jnp.where(
                group == source, jnp.take_along_axis(piece, lane, axis=1), value
            )
        found.append(value)

    x1, x2, x3 = [by_half(v) for v in velocity(point_ref[...])]
    ahead = x1 > 0
    upward = x2 > 0
    sigma = stream_x * jnp.abs(x1)
    sigma1 = 1.0 + sigma
    flux_y = stream_y * jnp.abs(x2)
    flux_z = stream_z * jnp.abs(x3)
    own = 1.0 - flux_y - flux_z
    row = sublane((8, LANES))
    first_plane = (row & 1) == 0
    lower = row < 4
    edge = jnp.where(ahead, ends_ref[0], ends_ref[1]) == 1

    ghosts = []
    for x in range(DEPTH):
        four = jnp.concatenate(
            [found[0][2 * x : 2 * x + 2], found[1][2 * x : 2 * x + 2]], axis=0
        )
        ghosts.append(jnp.concatenate([four, four], axis=0))

    for i in range(XROWS // 8):
        a, b, target = [], [], []
        for x in range(DEPTH):
            def column(q):
                at = DEPTH * q + x
                return jnp.broadcast_to(
                    columns[8 * i : 8 * i + 8, at : at + 1], (8, LANES)
                )

            base = x * XROWS + 8 * i
            f = f_ref[pl.ds(base, 8), :]
            c1, c2, c3 = x1 - column(0), x2 - column(1), x3 - column(2)
            square = c1 * c1 + c2 * c2 + c3 * c3
            along = c1 * column(3) + c2 * column(4) + c3 * column(5)
            ratio = square * column(6)
            shakhov = column(7) * jnp.exp(-0.5 * ratio) * (1.0 + along * (ratio - 5.0))
            rate = column(8)

            def ghost(wall):
                plane0, plane1 = wall_ref[x, wall, 0], wall_ref[x, wall, 1]
                mask = jnp.where(first_plane, plane0, plane1)
                return jnp.where(mask == 1, ghosts[x], shakhov)

            if i == 0:
                below = jnp.where(lower, ghost(0), pltpu.roll(f, 4, 0))
            else:
                below = f_ref[pl.ds(base - 4, 8), :]
            if i == XROWS // 8 - 1:
                above = jnp.where(lower, pltpu.roll(f, 4, 0), ghost(1))
            else:
                above = f_ref[pl.ds(base + 4, 8), :]
            upwind = jnp.where(upward, below, above)
            other = jnp.where(first_plane, pltpu.roll(f, 7, 0), pltpu.roll(f, 1, 0))
            inverse = 1.0 / (sigma1 + rate)
            a.append(sigma * inverse)
            b.append(
                (own * f + rate * shakhov + flux_y * upwind + flux_z * other) * inverse
            )
            target.append(shakhov)
        order = lambda v, t: jnp.where(ahead, v[t], v[DEPTH - 1 - t])
        a0 = order(a, 0)
        hold = order(b, 0) + jnp.where(edge, a0 * order(target, 0), 0.0)
        gain = jnp.where(edge, 0.0, a0)
        a_ref[pl.ds(8 * i, 8), :] = gain
        h_ref[pl.ds(8 * i, 8), :] = hold
        for t in range(1, DEPTH):
            at = order(a, t)
            gain = at * gain
            hold = at * hold + order(b, t)
            a_ref[pl.ds(t * XROWS + 8 * i, 8), :] = gain
            h_ref[pl.ds(t * XROWS + 8 * i, 8), :] = hold
        send_ref[2 * i] = jnp.where(lower, gain, pltpu.roll(hold, 4, 0))
        send_ref[2 * i + 1] = jnp.where(lower, pltpu.roll(gain, 4, 0), hold)


def chain_kernel(blocks, got_ref, point_ref, out_ref, keep_ref):
    ahead = (by_half(velocity(point_ref[...])[0]) > 0)[0:4]
    enter = jnp.zeros((4, LANES), F32)
    for k in range(blocks):
        keep_ref[k] = enter
        gain = jnp.where(ahead, got_ref[k, 0:4, :], got_ref[blocks - 1 - k, 0:4, :])
        hold = jnp.where(ahead, got_ref[k, 4:8, :], got_ref[blocks - 1 - k, 4:8, :])
        enter = gain * enter + hold
    for k in range(blocks):
        out_ref[k] = jnp.where(ahead, keep_ref[k], keep_ref[blocks - 1 - k])


def finish_kernel(enter_ref, a_ref, h_ref, point_ref, out_ref):
    ahead = by_half(velocity(point_ref[...])[0]) > 0
    for i in range(XROWS // 8):
        enter = enter_ref[pl.ds(8 * i, 8), :]
        value = []
        for t in range(DEPTH):
            at = pl.ds(t * XROWS + 8 * i, 8)
            value.append(a_ref[at, :] * enter + h_ref[at, :])
        for x in range(DEPTH):
            out_ref[pl.ds(x * XROWS + 8 * i, 8), :] = jnp.where(
                ahead, value[x], value[DEPTH - 1 - x]
            )


def call(kernel, shapes, scratch=(), scalars=0, inputs=0):
    specs = [pl.BlockSpec(memory_space=pltpu.SMEM)] * scalars
    specs += [pl.BlockSpec(memory_space=pltpu.VMEM)] * inputs
    outs = [jax.ShapeDtypeStruct(s, F32) for s in shapes]
    vmem = pl.BlockSpec(memory_space=pltpu.VMEM)
    single = len(outs) == 1
    return pl.pallas_call(
        kernel,
        out_shape=outs[0] if single else outs,
        in_specs=specs,
        out_specs=vmem if single else [vmem] * len(outs),
        scratch_shapes=list(scratch),
    )


def shards(distribution, wall_mask, grid_point, mirror_slot):
    blocks = lax.axis_size("space")
    here = lax.axis_index("space")
    ends = jnp.stack([here == 0, here == blocks - 1]).astype(jnp.int32)
    f = distribution.reshape(DEPTH, ROWS, PLANES, 2, LANES)
    f = f.transpose(0, 1, 3, 2, 4).reshape(DEPTH * XROWS, LANES)
    point = grid_point.reshape(2, LANES)
    mirror = mirror_slot.reshape(2, LANES)

    mine = call(moments_kernel, [(48, LANES)], inputs=2)(f, point)
    everyone = lax.all_gather(mine, "vel")
    send, gains, holds = call(
        blocks_kernel,
        [(ROWS, 8, LANES), (DEPTH * XROWS, LANES), (DEPTH * XROWS, LANES)],
        scalars=2,
        inputs=4,
    )(ends, wall_mask, everyone, f, point, mirror)
    chain = lax.all_to_all(send, "space", 0, 0, tiled=True)
    enters = call(
        lambda *refs: chain_kernel(blocks, *refs),
        [(ROWS, 4, LANES)],
        scratch=[pltpu.VMEM((ROWS, 4, LANES), F32)],
        inputs=2,
    )(chain, point)
    enter = lax.all_to_all(enters, "space", 0, 0, tiled=True)
    out = call(finish_kernel, [(DEPTH * XROWS, LANES)], inputs=4)(
        enter.reshape(XROWS, LANES), gains, holds, point
    )
    out = out.reshape(DEPTH, ROWS, 2, PLANES, LANES).transpose(0, 1, 3, 2, 4)
    return out.reshape(DEPTH, ROWS, PLANES, WIDTH)


def solution(mesh):
    placed = (P("space", None, None, "vel"), P("space", None, None), P("vel"), P("vel"))
    return jax.shard_map(
        shards, mesh=mesh, in_specs=placed, out_specs=P("space", None, None, "vel"), check_vma=False
    )
```

time: 486 us -> 69.1 us (0.14)
  the two profiles are of different devices: /device:TPU:198 before, /device:TPU:1 now
where the time goes in v1:
time: 69.1 us; the launch traced here: 68.5 us
  blocking collectives  57.7 us (84%)
  Pallas kernels  8.8 us (13%)
  local copies, waits for them, and re-layouts  1.36 us (2%)
    all_gather x1, blocking collectives, shards(): everyone = lax.all_gather(mine, 'vel')  23.6 us
    all_to_all x1, blocking collectives, shards(): chain = lax.all_to_all(send, 'space', 0, 0, tiled=True)  20.8 us
    all_to_all x1, blocking collectives, shards(): enter = lax.all_to_all(enters, 'space', 0, 0, tiled=True)  13.4 us
    pallas_call x1, Pallas kernels, shards(): call(blocks_kernel, [(ROWS, 8, LANES), (DEPTH * XROWS, LANES), (DEPTH * X...  3.22 us
    pallas_call x1, Pallas kernels, shards(): mine = call(moments_kernel, [(48, LANES)], inputs=2)(f, point)  2.15 us
    pallas_call x1, Pallas kernels, shards(): call(finish_kernel, [(DEPTH * XROWS, LANES)], inputs=4)  1.8 us
    pallas_call x1, Pallas kernels, shards(): call(lambda *refs: chain_kernel(blocks, *refs), [(ROWS, 4, LANES)], scrat...  1.63 us

profile of v1, /device:TPU:1, one launch (start us, length us, event | category | flops | bytes accessed | tf_op | source)
XLA Modules:
  0.0 68.5 jit_solution(10001130025429526923)
XLA Ops:
  0.0 0.0 copy-start
  0.0 0.7 copy-done
  0.7 0.7 copy.6.wall_ref
  1.4 2.2 %shard_map.46 = f32[48,128]{1,0:T(8,128)} custom-call(f32[512,128]{1,0:T(8,128)} %bitcast.17, s32[2,128]{1,0:T(2,128)} %bitcast.20), custom_call_target="tpu_custom_call" | custom-call | tf_op jit(solution)/shard_map/pallas_call | solution.py:259
  3.5 23.6 %all-gather = f32[768,128]{1,0:T(8,128)} all-gather(f32[48,128]{1,0:T(8,128)} %shard_map.46), channel_id=2, replica_groups=mesh['space'=32,'vel'=16] {'vel'}, dimensions={0}, use_global_device_ids=true | all-gather | bytes 417792 | tf_op jit(solution)/shard_map/all_gather | solution.py:260
  27.1 0.6 add_convert_fusion.ends_ref
  27.7 3.2 %shard_map.47 = (f32[32,8,128]{2,1,0:T(8,128)}, f32[512,128]{1,0:T(8,128)}, f32[512,128]{1,0:T(8,128)}) custom-call(s32[2]{0:T(128)} %add_convert_fusion.ends_ref, s32[4,2,2]{2,1,0:T(2,128)} %copy.6.wall_ref, f32[16,48,128]{2,1,0:T(8,128)} %bitcast.16, f32[512,128]{1,0:T(8,128)} %bitcast.18, s32[2,128]{1,0:T(2,128)} %bitcast.21, s32[2,128]{1,0:T(2,128)} %bitcast.24), custom_call_target="tpu_custom_call" | custom-call | tf_op jit(solution)/shard_map/pallas_call | solution.py:261
  30.9 20.8 %all_to_all.10.refs_0_ = f32[32,8,128]{2,1,0:T(8,128)} all-to-all(f32[32,8,128]{2,1,0:T(8,128)} %get-tuple-element.8), channel_id=1, replica_groups=mesh['space'=32,'vel'=16] {'space'}, dimensions={0} | all-to-all | bytes 262144 | tf_op jit(solution)/shard_map/all_to_all | solution.py:267
  51.7 1.6 %shard_map.48 = f32[32,4,128]{2,1,0:T(4,128)} custom-call(f32[32,8,128]{2,1,0:T(8,128)} %all_to_all.10.refs_0_, s32[2,128]{1,0:T(2,128)} %bitcast.22), custom_call_target="tpu_custom_call" | custom-call | tf_op jit(solution)/shard_map/pallas_call | solution.py:268
  53.3 13.4 %all_to_all.11 = f32[32,4,128]{2,1,0:T(4,128)} all-to-all(f32[32,4,128]{2,1,0:T(4,128)} %shard_map.48), channel_id=1, replica_groups=mesh['space'=32,'vel'=16] {'space'}, dimensions={0} | all-to-all | bytes 131072 | tf_op jit(solution)/shard_map/all_to_all | solution.py:274
  66.7 1.8 %shard_map.49 = f32[512,128]{1,0:T(8,128)} custom-call(f32[128,128]{1,0:T(8,128)} %bitcast.19, f32[512,128]{1,0:T(8,128)} %get-tuple-element.9.a_ref, f32[512,128]{1,0:T(8,128)} %get-tuple-element.10.h_ref, s32[2,128]{1,0:T(2,128)} %bitcast.23), custom_call_target="tpu_custom_call" | custom-call | tf_op jit(solution)/shard_map/pallas_call | solution.py:275
Async XLA Ops:
  0.0 0.7 copy-start

commit v2 on v1

--- a/solution.py
+++ b/solution.py
@@ -42,7 +42,26 @@
     return jnp.where((sublane((8, LANES)) & 2) == 0, low, high)
 
 
-def moments_kernel(f_ref, point_ref, out_ref):
+def moments_kernel(
+    f_hbm, point_hbm, mirror_hbm, wall_hbm,
+    out_ref, f_ref, pattern_ref, slot_ref,
+    point_ref, mirror_ref, wall_ref, f_sem, small_sem,
+):
+    small = [
+        pltpu.make_async_copy(src, dst, small_sem.at[k])
+        for k, (src, dst) in enumerate(
+            [(point_hbm, point_ref), (wall_hbm, wall_ref), (mirror_hbm, mirror_ref)]
+        )
+    ]
+    for copy in small:
+        copy.start()
+    chunks = []
+    for x in range(DEPTH):
+        rows = pl.ds(x * XROWS, XROWS)
+        chunks.append(pltpu.make_async_copy(f_hbm.at[rows], f_ref.at[rows], f_sem.at[x]))
+        chunks[x].start()
+
+    small[0].wait()
     points = point_ref[...]
     tables = []
     for half in range(2):
@@ -57,8 +76,22 @@
         ]
     table = jnp.concatenate(tables, axis=0)
     low_lane = (lax.broadcasted_iota(jnp.int32, (8, LANES), 1) & 2) == 0
-    x2 = velocity(points)[1]
+    pairs = velocity(points)
+    for k in range(3):
+        pattern_ref[k] = by_half(pairs[k])
+    small[1].wait()
     for x in range(DEPTH):
+        for wall in range(2):
+            planes = wall_ref[wall, :, x : x + 1].astype(F32)
+            planes = jnp.broadcast_to(planes, (PLANES, LANES))
+            pattern_ref[3 + 2 * x + wall] = jnp.concatenate([planes] * 4, axis=0)
+    small[2].wait()
+    for half in range(2):
+        slot_ref[half] = jnp.broadcast_to(mirror_ref[half : half + 1], (8, LANES))
+
+    x2 = pairs[1]
+    for x in range(DEPTH):
+        chunks[x].wait()
         sums = lax.dot_general(
             table,
             f_ref[pl.ds(x * XROWS, XROWS), :],
@@ -108,9 +141,7 @@
     return u + [h * scale for h in heat] + [inv_t, norm, rate]
 
 
-def blocks_kernel(
-    ends_ref, wall_ref, got_ref, f_ref, point_ref, mirror_ref, send_ref, a_ref, h_ref
-):
+def blocks_kernel(got_ref, f_ref, pattern_ref, slot_ref, send_ref, a_ref, h_ref):
     sums = got_ref[0, 0:32, :]
     for k in range(1, 16):
         sums = sums + got_ref[k, 0:32, :]
@@ -118,10 +149,9 @@
     filler = jnp.zeros((LANES - DEPTH * len(quantities), LANES), F32)
     columns = jnp.concatenate(quantities + [filler], axis=0).T
 
-    mirror = mirror_ref[...]
     found = []
     for half in range(2):
-        slot = jnp.broadcast_to(mirror[half : half + 1], (8, LANES))
+        slot = slot_ref[half]
         lane, group = slot & (LANES - 1), slot >> 7
         value = jnp.zeros((8, LANES), F32)
         for source in range(32):
@@ -131,7 +161,7 @@
             )
         found.append(value)
 
-    x1, x2, x3 = [by_half(v) for v in velocity(point_ref[...])]
+    x1, x2, x3 = pattern_ref[0], pattern_ref[1], pattern_ref[2]
     ahead = x1 > 0
     upward = x2 > 0
     sigma = stream_x * jnp.abs(x1)
@@ -142,7 +172,8 @@
     row = sublane((8, LANES))
     first_plane = (row & 1) == 0
     lower = row < 4
-    edge = jnp.where(ahead, ends_ref[0], ends_ref[1]) == 1
+    here = lax.axis_index("space")
+    edge = here == jnp.where(ahead, 0, lax.axis_size("space") - 1)
 
     ghosts = []
     for x in range(DEPTH):
@@ -170,9 +201,8 @@
             rate = column(8)
 
             def ghost(wall):
-                plane0, plane1 = wall_ref[x, wall, 0], wall_ref[x, wall, 1]
-                mask = jnp.where(first_plane, plane0, plane1)
-                return jnp.where(mask == 1, ghosts[x], shakhov)
+                mask = pattern_ref[3 + 2 * x + wall]
+                return jnp.where(mask == 1.0, ghosts[x], shakhov)
 
             if i == 0:
                 below = jnp.where(lower, ghost(0), pltpu.roll(f, 4, 0))
@@ -206,8 +236,8 @@
         send_ref[2 * i + 1] = jnp.where(lower, pltpu.roll(gain, 4, 0), hold)
 
 
-def chain_kernel(blocks, got_ref, point_ref, out_ref, keep_ref):
-    ahead = (by_half(velocity(point_ref[...])[0]) > 0)[0:4]
+def chain_kernel(blocks, got_ref, pattern_ref, out_ref, keep_ref):
+    ahead = pattern_ref[0, 0:4, :] > 0
     enter = jnp.zeros((4, LANES), F32)
     for k in range(blocks):
         keep_ref[k] = enter
@@ -218,63 +248,90 @@
         out_ref[k] = jnp.where(ahead, keep_ref[k], keep_ref[blocks - 1 - k])
 
 
-def finish_kernel(enter_ref, a_ref, h_ref, point_ref, out_ref):
-    ahead = by_half(velocity(point_ref[...])[0]) > 0
-    for i in range(XROWS // 8):
-        enter = enter_ref[pl.ds(8 * i, 8), :]
-        value = []
-        for t in range(DEPTH):
-            at = pl.ds(t * XROWS + 8 * i, 8)
-            value.append(a_ref[at, :] * enter + h_ref[at, :])
-        for x in range(DEPTH):
-            out_ref[pl.ds(x * XROWS + 8 * i, 8), :] = jnp.where(
-                ahead, value[x], value[DEPTH - 1 - x]
-            )
-
-
-def call(kernel, shapes, scratch=(), scalars=0, inputs=0):
-    specs = [pl.BlockSpec(memory_space=pltpu.SMEM)] * scalars
-    specs += [pl.BlockSpec(memory_space=pltpu.VMEM)] * inputs
-    outs = [jax.ShapeDtypeStruct(s, F32) for s in shapes]
-    vmem = pl.BlockSpec(memory_space=pltpu.VMEM)
-    single = len(outs) == 1
-    return pl.pallas_call(
-        kernel,
-        out_shape=outs[0] if single else outs,
-        in_specs=specs,
-        out_specs=vmem if single else [vmem] * len(outs),
-        scratch_shapes=list(scratch),
-    )
+def finish_kernel(enter_ref, a_ref, h_ref, pattern_ref, out_hbm, out_ref, sem):
+    ahead = pattern_ref[0] > 0
+    copies = []
+    for x, mate in ((0, DEPTH - 1), (1, DEPTH - 2)):
+        for i in range(XROWS // 8):
+            enter = enter_ref[pl.ds(8 * i, 8), :]
+            value = []
+            for t in (x, mate):
+                at = pl.ds(t * XROWS + 8 * i, 8)
+                value.append(a_ref[at, :] * enter + h_ref[at, :])
+            out_ref[pl.ds(x * XROWS + 8 * i, 8), :] = jnp.where(ahead, value[0], value[1])
+            out_ref[pl.ds(mate * XROWS + 8 * i, 8), :] = jnp.where(ahead, value[1], value[0])
+        for t in (x, mate):
+            rows = pl.ds(t * XROWS, XROWS)
+            copies.append(pltpu.make_async_copy(out_ref.at[rows], out_hbm.at[rows], sem.at[t]))
+            copies[-1].start()
+    for copy in copies:
+        copy.wait()
+
+
+ON_CHIP = pl.BlockSpec(memory_space=pltpu.VMEM)
+ANYWHERE = pl.BlockSpec(memory_space=pl.ANY)
+
+
+def held(x):
+    return pltpu.with_memory_space_constraint(x, pltpu.VMEM)
 
 
 def shards(distribution, wall_mask, grid_point, mirror_slot):
     blocks = lax.axis_size("space")
-    here = lax.axis_index("space")
-    ends = jnp.stack([here == 0, here == blocks - 1]).astype(jnp.int32)
     f = distribution.reshape(DEPTH, ROWS, PLANES, 2, LANES)
     f = f.transpose(0, 1, 3, 2, 4).reshape(DEPTH * XROWS, LANES)
     point = grid_point.reshape(2, LANES)
     mirror = mirror_slot.reshape(2, LANES)
-
-    mine = call(moments_kernel, [(48, LANES)], inputs=2)(f, point)
+    wall = wall_mask.transpose(1, 2, 0)
+
+    mine, kept, pattern, slots = pl.pallas_call(
+        moments_kernel,
+        out_shape=[
+            pltpu.VMEM((48, LANES), F32),
+            pltpu.VMEM((DEPTH * XROWS, LANES), F32),
+            pltpu.VMEM((3 + 2 * DEPTH, 8, LANES), F32),
+            pltpu.VMEM((2, 8, LANES), jnp.int32),
+        ],
+        in_specs=[ANYWHERE] * 4,
+        out_specs=[ON_CHIP] * 4,
+        scratch_shapes=[
+            pltpu.VMEM((2, LANES), jnp.int32),
+            pltpu.VMEM((2, LANES), jnp.int32),
+            pltpu.VMEM((2, PLANES, DEPTH), jnp.int32),
+            pltpu.SemaphoreType.DMA((DEPTH,)),
+            pltpu.SemaphoreType.DMA((3,)),
+        ],
+    )(f, point, mirror, wall)
     everyone = lax.all_gather(mine, "vel")
-    send, gains, holds = call(
+    send, gains, holds = pl.pallas_call(
         blocks_kernel,
-        [(ROWS, 8, LANES), (DEPTH * XROWS, LANES), (DEPTH * XROWS, LANES)],
-        scalars=2,
-        inputs=4,
-    )(ends, wall_mask, everyone, f, point, mirror)
+        out_shape=[
+            pltpu.VMEM((ROWS, 8, LANES), F32),
+            pltpu.VMEM((DEPTH * XROWS, LANES), F32),
+            pltpu.VMEM((DEPTH * XROWS, LANES), F32),
+        ],
+        in_specs=[ON_CHIP] * 4,
+        out_specs=[ON_CHIP] * 3,
+    )(held(everyone), held(kept), held(pattern), held(slots))
     chain = lax.all_to_all(send, "space", 0, 0, tiled=True)
-    enters = call(
+    enters = pl.pallas_call(
         lambda *refs: chain_kernel(blocks, *refs),
-        [(ROWS, 4, LANES)],
-        scratch=[pltpu.VMEM((ROWS, 4, LANES), F32)],
-        inputs=2,
-    )(chain, point)
+        out_shape=pltpu.VMEM((ROWS, 4, LANES), F32),
+        in_specs=[ON_CHIP] * 2,
+        out_specs=ON_CHIP,
+        scratch_shapes=[pltpu.VMEM((ROWS, 4, LANES), F32)],
+    )(held(chain), held(pattern))
     enter = lax.all_to_all(enters, "space", 0, 0, tiled=True)
-    out = call(finish_kernel, [(DEPTH * XROWS, LANES)], inputs=4)(
-        enter.reshape(XROWS, LANES), gains, holds, point
-    )
+    out = pl.pallas_call(
+        finish_kernel,
+        out_shape=jax.ShapeDtypeStruct((DEPTH * XROWS, LANES), F32),
+        in_specs=[ON_CHIP] * 4,
+        out_specs=ANYWHERE,
+        scratch_shapes=[
+            pltpu.VMEM((DEPTH * XROWS, LANES), F32),
+            pltpu.SemaphoreType.DMA((DEPTH,)),
+        ],
+    )(held(enter.reshape(XROWS, LANES)), held(gains), held(holds), held(pattern))
     out = out.reshape(DEPTH, ROWS, 2, PLANES, LANES).transpose(0, 1, 3, 2, 4)
     return out.reshape(DEPTH, ROWS, PLANES, WIDTH)
 

time: 69.1 us -> 59.8 us (0.87)
  Pallas kernels: 8.8 us -> 4.63 us
  blocking collectives: 57.7 us -> 54.7 us
  local copies, waits for them, and re-layouts: 1.36 us -> 0 us
    pallas_call x4, Pallas kernels: 8.8 us -> 4.63 us  [the longest x1 2.47 us: shards(): pl.pallas_call(moments_kernel, out_shape=[pltpu.VMEM((48, LANES), F32), p...]
    all_gather x1, blocking collectives: 23.6 us -> 22 us  [shards(): everyone = lax.all_gather(mine, 'vel')]
    unnamed x3 -> x0, local copies, waits for them, and re-layouts: 1.36 us -> none
    all_to_all x1, blocking collectives: 13.4 us -> 12.2 us  [shards(): enter = lax.all_to_all(enters, 'space', 0, 0, tiled=True)]
where the time goes in v2:
time: 59.8 us; the launch traced here: 59.3 us
  blocking collectives  54.7 us (91%)
  Pallas kernels  4.63 us (8%)
    all_gather x1, blocking collectives, shards(): everyone = lax.all_gather(mine, 'vel')  22 us
    all_to_all x1, blocking collectives, shards(): chain = lax.all_to_all(send, 'space', 0, 0, tiled=True)  20.5 us
    all_to_all x1, blocking collectives, shards(): enter = lax.all_to_all(enters, 'space', 0, 0, tiled=True)  12.2 us
    pallas_call x1, Pallas kernels, shards(): pl.pallas_call(moments_kernel, out_shape=[pltpu.VMEM((48, LANES), F32), p...  2.47 us
    pallas_call x1, Pallas kernels, shards(): pl.pallas_call(blocks_kernel, out_shape=[pltpu.VMEM((ROWS, 8, LANES), F32...  1.32 us

profile of v2, /device:TPU:1, one launch (start us, length us, event | category | flops | bytes accessed | tf_op | source)
XLA Modules:
  0.0 59.3 jit_solution(6578515498606629420)
XLA Ops:
  0.0 2.5 %shard_map.46 = (f32[48,128]{1,0:T(8,128)S(1)}, f32[512,128]{1,0:T(8,128)S(1)}, f32[11,8,128]{2,1,0:T(8,128)S(1)}, s32[2,8,128]{2,1,0:T(8,128)S(1)}) custom-call(f32[512,128]{1,0:T(8,128)} %bitcast.17, s32[2,128]{1,0:T(2,128)} %bitcast.19, s32[2,128]{1,0:T(2,128)} %bitcast.20, s32[2,2,4]{2,1,0:T(2,128)} %bitcast.18), custom_call_target="tpu_custom_call" | custom-call | tf_op jit(solution)/shard_map/pallas_call | solution.py:287
  2.5 22.0 %all-gather = f32[768,128]{1,0:T(8,128)S(1)} all-gather(f32[48,128]{1,0:T(8,128)S(1)} %get-tuple-element.12), channel_id=2, replica_groups=mesh['space'=32,'vel'=16] {'vel'}, dimensions={0}, use_global_device_ids=true | all-gather | bytes 417792 | tf_op jit(solution)/shard_map/all_gather | solution.py:305
  24.4 1.3 %shard_map.47 = (f32[32,8,128]{2,1,0:T(8,128)S(1)}, f32[512,128]{1,0:T(8,128)S(1)}, f32[512,128]{1,0:T(8,128)S(1)}) custom-call(f32[16,48,128]{2,1,0:T(8,128)S(1)} %bitcast.15, f32[512,128]{1,0:T(8,128)S(1)} %get-tuple-element.13.f_ref, f32[11,8,128]{2,1,0:T(8,128)S(1)} %get-tuple-element.14.pattern_ref.refs_1_, s32[2,8,128]{2,1,0:T(8,128)S(1)} %get-tuple-element.15.slot_ref), custom_call_target="tpu_custom_call" | custom-call | tf_op jit(solution)/shard_map/pallas_call | solution.py:306
  25.8 20.5 %all_to_all.10.refs_0_ = f32[32,8,128]{2,1,0:T(8,128)S(1)} all-to-all(f32[32,8,128]{2,1,0:T(8,128)S(1)} %get-tuple-element.16), channel_id=1, replica_groups=mesh['space'=32,'vel'=16] {'space'}, dimensions={0} | all-to-all | bytes 262144 | tf_op jit(solution)/shard_map/all_to_all | solution.py:316
  46.2 0.1 shard_map.48
  46.3 12.2 %all_to_all.11 = f32[32,4,128]{2,1,0:T(4,128)S(1)} all-to-all(f32[32,4,128]{2,1,0:T(4,128)S(1)} %shard_map.48), channel_id=1, replica_groups=mesh['space'=32,'vel'=16] {'space'}, dimensions={0} | all-to-all | bytes 131072 | tf_op jit(solution)/shard_map/all_to_all | solution.py:324
  58.5 0.8 %shard_map.49 = f32[512,128]{1,0:T(8,128)} custom-call(f32[128,128]{1,0:T(8,128)S(1)} %bitcast.16, f32[512,128]{1,0:T(8,128)S(1)} %get-tuple-element.17.a_ref, f32[512,128]{1,0:T(8,128)S(1)} %get-tuple-element.18.h_ref, f32[11,8,128]{2,1,0:T(8,128)S(1)} %get-tuple-element.14.pattern_ref.refs_1_), custom_call_target="tpu_custom_call" | custom-call | tf_op jit(solution)/shard_map/pallas_call | solution.py:325

commit v3 on v2

--- a/solution.py
+++ b/solution.py
@@ -23,6 +23,9 @@
 LANES = 128
 XROWS = ROWS * 2 * PLANES
 F32 = jnp.float32
+
+CHUNKS = 8
+CHUNK_ROWS = 17
 
 
 def velocity(points):
@@ -141,13 +144,26 @@
     return u + [h * scale for h in heat] + [inv_t, norm, rate]
 
 
-def blocks_kernel(got_ref, f_ref, pattern_ref, slot_ref, send_ref, a_ref, h_ref):
+def blocks_kernel(copies, got_ref, f_ref, pattern_ref, slot_ref, send_ref, a_ref, h_ref):
     sums = got_ref[0, 0:32, :]
     for k in range(1, 16):
         sums = sums + got_ref[k, 0:32, :]
     quantities = cell_quantities(sums)
     filler = jnp.zeros((LANES - DEPTH * len(quantities), LANES), F32)
     columns = jnp.concatenate(quantities + [filler], axis=0).T
+
+    lane = lax.broadcasted_iota(jnp.int32, (8, LANES), 1)
+    cell = (lane >> 3) & 7
+    source = 16 * sublane((8, LANES)) + 4 * (cell >> 1) + (cell & 1)
+    speed = stream_x * SPACING * ((lane & 7).astype(F32) + 0.5)
+    chunk_gain = jnp.ones((8, LANES), F32)
+    for x in range(DEPTH):
+        rate = jnp.broadcast_to(quantities[8][x : x + 1], (8, LANES))
+        rate = jnp.take_along_axis(rate, source, axis=1)
+        chunk_gain = chunk_gain * (speed / (1.0 + speed + rate))
+    for to in range(copies * CHUNKS):
+        at = to % CHUNKS
+        send_ref[pl.ds(CHUNK_ROWS * to + 16, 1), :] = chunk_gain[at : at + 1]
 
     found = []
     for half in range(2):
@@ -232,20 +248,39 @@
             hold = at * hold + order(b, t)
             a_ref[pl.ds(t * XROWS + 8 * i, 8), :] = gain
             h_ref[pl.ds(t * XROWS + 8 * i, 8), :] = hold
-        send_ref[2 * i] = jnp.where(lower, gain, pltpu.roll(hold, 4, 0))
-        send_ref[2 * i + 1] = jnp.where(lower, pltpu.roll(gain, 4, 0), hold)
-
-
-def chain_kernel(blocks, got_ref, pattern_ref, out_ref, keep_ref):
-    ahead = pattern_ref[0, 0:4, :] > 0
-    enter = jnp.zeros((4, LANES), F32)
-    for k in range(blocks):
-        keep_ref[k] = enter
-        gain = jnp.where(ahead, got_ref[k, 0:4, :], got_ref[blocks - 1 - k, 0:4, :])
-        hold = jnp.where(ahead, got_ref[k, 4:8, :], got_ref[blocks - 1 - k, 4:8, :])
-        enter = gain * enter + hold
-    for k in range(blocks):
-        out_ref[k] = jnp.where(ahead, keep_ref[k], keep_ref[blocks - 1 - k])
+        for copy in range(copies):
+            to = copy * CHUNKS + i // 2
+            send_ref[pl.ds(CHUNK_ROWS * to + 8 * (i % 2), 8), :] = hold
+
+
+def chain_kernel(copies, got_ref, pattern_ref, out_ref, gain_ref, keep_ref):
+    blocks = copies * CHUNKS
+    ahead = pattern_ref[0] > 0
+    which = (jnp.abs(pattern_ref[0]) * (1.0 / SPACING) - 0.5).astype(jnp.int32)
+    row = sublane((8, LANES))
+    for half in range(2):
+        cell = 2 * (2 * half + (row >> 2)) + (row & 1)
+        source = 8 * cell + which
+        for k in range(blocks):
+            gain = jnp.broadcast_to(got_ref[pl.ds(CHUNK_ROWS * k + 16, 1), :], (8, LANES))
+            gain_ref[k] = jnp.take_along_axis(gain, source, axis=1)
+        enter = jnp.zeros((8, LANES), F32)
+        for k in range(blocks):
+            keep_ref[half, k] = enter
+            back = blocks - 1 - k
+            gain = jnp.where(ahead, gain_ref[k], gain_ref[back])
+            hold = jnp.where(
+                ahead,
+                got_ref[pl.ds(CHUNK_ROWS * k + 8 * half, 8), :],
+                got_ref[pl.ds(CHUNK_ROWS * back + 8 * half, 8), :],
+            )
+            enter = gain * enter + hold
+    first = lax.axis_index("space") // CHUNKS * CHUNKS
+    for half in range(2):
+        for x in range(CHUNKS):
+            out_ref[x, pl.ds(8 * half, 8), :] = jnp.where(
+                ahead, keep_ref[half, first + x], keep_ref[half, blocks - 1 - x - first]
+            )
 
 
 def finish_kernel(enter_ref, a_ref, h_ref, pattern_ref, out_hbm, out_ref, sem):
@@ -278,6 +313,7 @@
 
 def shards(distribution, wall_mask, grid_point, mirror_slot):
     blocks = lax.axis_size("space")
+    copies = blocks // CHUNKS
     f = distribution.reshape(DEPTH, ROWS, PLANES, 2, LANES)
     f = f.transpose(0, 1, 3, 2, 4).reshape(DEPTH * XROWS, LANES)
     point = grid_point.reshape(2, LANES)
@@ -304,24 +340,30 @@
     )(f, point, mirror, wall)
     everyone = lax.all_gather(mine, "vel")
     send, gains, holds = pl.pallas_call(
-        blocks_kernel,
+        lambda *refs: blocks_kernel(copies, *refs),
         out_shape=[
-            pltpu.VMEM((ROWS, 8, LANES), F32),
+            pltpu.VMEM((blocks * CHUNK_ROWS, LANES), F32),
             pltpu.VMEM((DEPTH * XROWS, LANES), F32),
             pltpu.VMEM((DEPTH * XROWS, LANES), F32),
         ],
         in_specs=[ON_CHIP] * 4,
         out_specs=[ON_CHIP] * 3,
     )(held(everyone), held(kept), held(pattern), held(slots))
-    chain = lax.all_to_all(send, "space", 0, 0, tiled=True)
+    chain = lax.all_to_all(
+        send.reshape(blocks, 1, CHUNK_ROWS * LANES), "space", 0, 0, tiled=True
+    ).reshape(blocks * CHUNK_ROWS, LANES)
     enters = pl.pallas_call(
-        lambda *refs: chain_kernel(blocks, *refs),
-        out_shape=pltpu.VMEM((ROWS, 4, LANES), F32),
+        lambda *refs: chain_kernel(copies, *refs),
+        out_shape=pltpu.VMEM((CHUNKS, 16, LANES), F32),
         in_specs=[ON_CHIP] * 2,
         out_specs=ON_CHIP,
-        scratch_shapes=[pltpu.VMEM((ROWS, 4, LANES), F32)],
+        scratch_shapes=[
+            pltpu.VMEM((blocks, 8, LANES), F32),
+            pltpu.VMEM((2, blocks, 8, LANES), F32),
+        ],
     )(held(chain), held(pattern))
-    enter = lax.all_to_all(enters, "space", 0, 0, tiled=True)
+    lines = [[CHUNKS * z + x for x in range(CHUNKS)] for z in range(copies)]
+    enter = lax.all_to_all(enters, "space", 0, 0, axis_index_groups=lines, tiled=True)
     out = pl.pallas_call(
         finish_kernel,
         out_shape=jax.ShapeDtypeStruct((DEPTH * XROWS, LANES), F32),

time: 59.8 us -> 58.5 us (0.978)
  blocking collectives: 54.7 us -> 53 us
    all_to_all x2, blocking collectives: 32.7 us -> 31.1 us  [the longest x1 22.8 us: shards(): lax.all_to_all(send.reshape(blocks, 1, CHUNK_ROWS * LANES), 'space', 0, 0...]
where the time goes in v3:
time: 58.5 us; the launch traced here: 57.8 us
  blocking collectives  53 us (91%)
  Pallas kernels  4.78 us (8%)
    all_to_all x1, blocking collectives, shards(): lax.all_to_all(send.reshape(blocks, 1, CHUNK_ROWS * LANES), 'space', 0, 0...  22.8 us
    all_gather x1, blocking collectives, shards(): everyone = lax.all_gather(mine, 'vel')  22 us
    all_to_all x1, blocking collectives, shards(): lax.all_to_all(enters, 'space', 0, 0, axis_index_groups=lines, tiled=True)  8.25 us
    pallas_call x1, Pallas kernels, shards(): pl.pallas_call(moments_kernel, out_shape=[pltpu.VMEM((48, LANES), F32), p...  2.47 us
    pallas_call x1, Pallas kernels, shards(): pl.pallas_call(lambda *refs: blocks_kernel(copies, *refs), out_shape=[plt...  1.32 us

profile of v3, /device:TPU:1, one launch (start us, length us, event | category | flops | bytes accessed | tf_op | source)
XLA Modules:
  0.0 57.8 jit_solution(8070136514346414476)
XLA Ops:
  0.0 2.5 %shard_map.46 = (f32[48,128]{1,0:T(8,128)S(1)}, f32[512,128]{1,0:T(8,128)S(1)}, f32[11,8,128]{2,1,0:T(8,128)S(1)}, s32[2,8,128]{2,1,0:T(8,128)S(1)}) custom-call(f32[512,128]{1,0:T(8,128)} %bitcast.21, s32[2,128]{1,0:T(2,128)} %bitcast.23, s32[2,128]{1,0:T(2,128)} %bitcast.24, s32[2,2,4]{2,1,0:T(2,128)} %bitcast.22), custom_call_target="tpu_custom_call" | custom-call | tf_op jit(solution)/shard_map/pallas_call | solution.py:323
  2.5 22.0 %all-gather = f32[768,128]{1,0:T(8,128)S(1)} all-gather(f32[48,128]{1,0:T(8,128)S(1)} %get-tuple-element.12), channel_id=2, replica_groups=mesh['space'=32,'vel'=16] {'vel'}, dimensions={0}, use_global_device_ids=true | all-gather | bytes 417792 | tf_op jit(solution)/shard_map/all_gather | solution.py:341
  24.4 1.3 %shard_map.47 = (f32[544,128]{1,0:T(8,128)S(1)}, f32[512,128]{1,0:T(8,128)S(1)}, f32[512,128]{1,0:T(8,128)S(1)}) custom-call(f32[16,48,128]{2,1,0:T(8,128)S(1)} %bitcast.17, f32[512,128]{1,0:T(8,128)S(1)} %get-tuple-element.13.refs_1_, f32[11,8,128]{2,1,0:T(8,128)S(1)} %get-tuple-element.14.refs_2_.refs_1_.pattern_ref, ...), custom_call_target="tpu_custom_call" | custom-call | tf_op jit(solution)/shard_map/pallas_call | solution.py:342
  25.8 22.8 %all_to_all.10 = f32[32,1,2176]{2,1,0:T(1,128)S(1)} all-to-all(f32[32,1,2176]{2,1,0:T(1,128)S(1)} %bitcast.19), channel_id=1, replica_groups=mesh['space'=32,'vel'=16] {'space'}, dimensions={0} | all-to-all | bytes 557056 | tf_op jit(solution)/shard_map/all_to_all | solution.py:352
  48.6 0.2 shard_map.48
  48.8 8.3 %all_to_all.11 = f32[8,16,128]{2,1,0:T(8,128)S(1)} all-to-all(f32[8,16,128]{2,1,0:T(8,128)S(1)} %shard_map.48), channel_id=1, replica_groups={{0,16,32,48,64,80,96,112},{128,144,160,176,192,208,224,240},{256,272,28..., dimensions={0} | all-to-all | bytes 131072 | tf_op jit(solution)/shard_map/all_to_all | solution.py:366
  57.1 0.8 %shard_map.49 = f32[512,128]{1,0:T(8,128)} custom-call(f32[128,128]{1,0:T(8,128)S(1)} %bitcast.20, f32[512,128]{1,0:T(8,128)S(1)} %get-tuple-element.17.a_ref, f32[512,128]{1,0:T(8,128)S(1)} %get-tuple-element.18.h_ref, f32[11,8,128]{2,1,0:T(8,128)S(1)} %get-tuple-element.14.refs_2_.refs_1_.pattern_ref), custom_call_target="tpu_custom_call" | custom-call | tf_op jit(solution)/shard_map/pallas_call | solution.py:367

commit v4 on v3

--- a/solution.py
+++ b/solution.py
@@ -23,6 +23,7 @@
 LANES = 128
 XROWS = ROWS * 2 * PLANES
 F32 = jnp.float32
+BF16 = jnp.bfloat16
 
 CHUNKS = 8
 CHUNK_ROWS = 17
@@ -59,8 +60,8 @@
     for copy in small:
         copy.start()
     chunks = []
-    for x in range(DEPTH):
-        rows = pl.ds(x * XROWS, XROWS)
+    for x in range(2):
+        rows = pl.ds(2 * x * XROWS, 2 * XROWS)
         chunks.append(pltpu.make_async_copy(f_hbm.at[rows], f_ref.at[rows], f_sem.at[x]))
         chunks[x].start()
 
@@ -70,14 +71,16 @@
     for half in range(2):
         x1, x2, x3 = velocity(points[half : half + 1])
         square = x1 * x1 + x2 * x2 + x3 * x3
-        zero = jnp.zeros_like(x1)
+        cubes = [x1 * square, x2 * square, x3 * square]
+        coarse = [c.astype(BF16).astype(F32) for c in cubes]
         tables += [
             jnp.ones_like(x1), x1, x2, x3,
             x1 * x1, x2 * x2, x3 * x3, x1 * x2,
-            x1 * x3, x2 * x3, x1 * square, x2 * square,
-            x3 * square, zero, zero, zero,
+            x1 * x3, x2 * x3, *coarse,
+            *[c - r for c, r in zip(cubes, coarse)],
         ]
-    table = jnp.concatenate(tables, axis=0)
+    table = jnp.concatenate(tables, axis=0).astype(BF16)
+    table = jnp.concatenate([table] * 3, axis=1)
     low_lane = (lax.broadcasted_iota(jnp.int32, (8, LANES), 1) & 2) == 0
     pairs = velocity(points)
     for k in range(3):
@@ -94,14 +97,20 @@
 
     x2 = pairs[1]
     for x in range(DEPTH):
-        chunks[x].wait()
-        sums = lax.dot_general(
-            table,
-            f_ref[pl.ds(x * XROWS, XROWS), :],
-            (((1,), (1,)), ((), ())),
-            precision=lax.Precision.HIGHEST,
-            preferred_element_type=F32,
-        )
+        if x % 2 == 0:
+            chunks[x // 2].wait()
+            f = f_ref[pl.ds(x * XROWS, 2 * XROWS), :]
+            high = f.astype(BF16)
+            rest = f - high.astype(F32)
+            middle = rest.astype(BF16)
+            low = (rest - middle.astype(F32)).astype(BF16)
+            both = lax.dot_general(
+                table,
+                jnp.concatenate([high, middle, low], axis=1),
+                (((1,), (1,)), ((), ())),
+                preferred_element_type=F32,
+            )
+        sums = both[:, XROWS * (x % 2) : XROWS * (x % 2 + 1)]
         packed = jnp.where(
             low_lane,
             sums[0:8] + pltpu.roll(sums[16:24], LANES - 2, 1),
@@ -135,7 +144,7 @@
     heat = []
     for k in range(3):
         cross = sum(u[j] * pressure[min(j, k), max(j, k)] for j in range(3))
-        heat.append(0.5 * (high[2 + k] - 2.0 * cross + u[k] * (2.0 * n * speed - energy)))
+        heat.append(0.5 * (high[2 + k] + high[5 + k] - 2.0 * cross + u[k] * (2.0 * n * speed - energy)))
     inv_t = 1.0 / temperature
     scale = (1.0 - diffusivity_ratio) / 5.0 * inv * inv_t * inv_t
     arg = 2.0 * math.pi * temperature
@@ -334,7 +343,7 @@
             pltpu.VMEM((2, LANES), jnp.int32),
             pltpu.VMEM((2, LANES), jnp.int32),
             pltpu.VMEM((2, PLANES, DEPTH), jnp.int32),
-            pltpu.SemaphoreType.DMA((DEPTH,)),
+            pltpu.SemaphoreType.DMA((2,)),
             pltpu.SemaphoreType.DMA((3,)),
         ],
     )(f, point, mirror, wall)

time: 58.5 us -> 57.6 us (0.985)
  Pallas kernels: 4.78 us -> 3.87 us
    pallas_call x1, Pallas kernels: 2.47 us -> 1.57 us  [shards(): pl.pallas_call(moments_kernel, out_shape=[pltpu.VMEM((48, LANES), F32), p...]
where the time goes in v4:
time: 57.6 us; the launch traced here: 56.9 us
  blocking collectives  53 us (92%)
  Pallas kernels  3.87 us (7%)
    all_to_all x1, blocking collectives, shards(): lax.all_to_all(send.reshape(blocks, 1, CHUNK_ROWS * LANES), 'space', 0, 0...  22.8 us
    all_gather x1, blocking collectives, shards(): everyone = lax.all_gather(mine, 'vel')  22 us
    all_to_all x1, blocking collectives, shards(): lax.all_to_all(enters, 'space', 0, 0, axis_index_groups=lines, tiled=True)  8.25 us
    pallas_call x1, Pallas kernels, shards(): pl.pallas_call(moments_kernel, out_shape=[pltpu.VMEM((48, LANES), F32), p...  1.57 us
    pallas_call x1, Pallas kernels, shards(): pl.pallas_call(lambda *refs: blocks_kernel(copies, *refs), out_shape=[plt...  1.31 us

profile of v4, /device:TPU:1, one launch (start us, length us, event | category | flops | bytes accessed | tf_op | source)
XLA Modules:
  0.0 56.9 jit_solution(12275621204520482578)
XLA Ops:
  0.0 1.6 %shard_map.46 = (f32[48,128]{1,0:T(8,128)S(1)}, f32[512,128]{1,0:T(8,128)S(1)}, f32[11,8,128]{2,1,0:T(8,128)S(1)}, s32[2,8,128]{2,1,0:T(8,128)S(1)}) custom-call(f32[512,128]{1,0:T(8,128)} %bitcast.21, s32[2,128]{1,0:T(2,128)} %bitcast.23, s32[2,128]{1,0:T(2,128)} %bitcast.24, s32[2,2,4]{2,1,0:T(2,128)} %bitcast.22), custom_call_target="tpu_custom_call" | custom-call | tf_op jit(solution)/shard_map/pallas_call | solution.py:332
  1.6 22.0 %all-gather = f32[768,128]{1,0:T(8,128)S(1)} all-gather(f32[48,128]{1,0:T(8,128)S(1)} %get-tuple-element.12), channel_id=2, replica_groups=mesh['space'=32,'vel'=16] {'vel'}, dimensions={0}, use_global_device_ids=true | all-gather | bytes 417792 | tf_op jit(solution)/shard_map/all_gather | solution.py:350
  23.5 1.3 %shard_map.47 = (f32[544,128]{1,0:T(8,128)S(1)}, f32[512,128]{1,0:T(8,128)S(1)}, f32[512,128]{1,0:T(8,128)S(1)}) custom-call(f32[16,48,128]{2,1,0:T(8,128)S(1)} %bitcast.17, f32[512,128]{1,0:T(8,128)S(1)} %get-tuple-element.13.refs_1_, f32[11,8,128]{2,1,0:T(8,128)S(1)} %get-tuple-element.14.refs_2_.refs_1_.pattern_ref, ...), custom_call_target="tpu_custom_call" | custom-call | tf_op jit(solution)/shard_map/pallas_call | solution.py:351
  24.9 22.8 %all_to_all.10 = f32[32,1,2176]{2,1,0:T(1,128)S(1)} all-to-all(f32[32,1,2176]{2,1,0:T(1,128)S(1)} %bitcast.19), channel_id=1, replica_groups=mesh['space'=32,'vel'=16] {'space'}, dimensions={0} | all-to-all | bytes 557056 | tf_op jit(solution)/shard_map/all_to_all | solution.py:361
  47.7 0.2 shard_map.48
  47.9 8.3 %all_to_all.11 = f32[8,16,128]{2,1,0:T(8,128)S(1)} all-to-all(f32[8,16,128]{2,1,0:T(8,128)S(1)} %shard_map.48), channel_id=1, replica_groups={{0,16,32,48,64,80,96,112},{128,144,160,176,192,208,224,240},{256,272,28..., dimensions={0} | all-to-all | bytes 131072 | tf_op jit(solution)/shard_map/all_to_all | solution.py:375
  56.2 0.8 %shard_map.49 = f32[512,128]{1,0:T(8,128)} custom-call(f32[128,128]{1,0:T(8,128)S(1)} %bitcast.20, f32[512,128]{1,0:T(8,128)S(1)} %get-tuple-element.17.a_ref, f32[512,128]{1,0:T(8,128)S(1)} %get-tuple-element.18.h_ref, f32[11,8,128]{2,1,0:T(8,128)S(1)} %get-tuple-element.14.refs_2_.refs_1_.pattern_ref), custom_call_target="tpu_custom_call" | custom-call | tf_op jit(solution)/shard_map/pallas_call | solution.py:376

commit v5 on v4

--- a/solution.py
+++ b/solution.py
@@ -28,6 +28,8 @@
 CHUNKS = 8
 CHUNK_ROWS = 17
 
+SHARE = 23
+
 
 def velocity(points):
     first = (points >> 8).astype(F32)
@@ -48,8 +50,8 @@
 
 def moments_kernel(
     f_hbm, point_hbm, mirror_hbm, wall_hbm,
-    out_ref, f_ref, pattern_ref, slot_ref,
-    point_ref, mirror_ref, wall_ref, f_sem, small_sem,
+    send_ref, f_ref, pattern_ref,
+    half_ref, point_ref, mirror_ref, wall_ref, f_sem, small_sem,
 ):
     small = [
         pltpu.make_async_copy(src, dst, small_sem.at[k])
@@ -92,8 +94,8 @@
             planes = jnp.broadcast_to(planes, (PLANES, LANES))
             pattern_ref[3 + 2 * x + wall] = jnp.concatenate([planes] * 4, axis=0)
     small[2].wait()
-    for half in range(2):
-        slot_ref[half] = jnp.broadcast_to(mirror_ref[half : half + 1], (8, LANES))
+    for core in range(2):
+        half_ref[core, 21:23, :] = mirror_ref[...].astype(F32)
 
     x2 = pairs[1]
     for x in range(DEPTH):
@@ -116,23 +118,45 @@
             sums[0:8] + pltpu.roll(sums[16:24], LANES - 2, 1),
             sums[24:32] + pltpu.roll(sums[8:16], 2, 1),
         )
-        out_ref[pl.ds(x, 8, stride=DEPTH), :] = packed
+        core, second = divmod(x, 2)
+        tail = packed[5:8]
+        half_ref[core, pl.ds(5 * second, 2), :] = packed[0:2]
+        half_ref[core, pl.ds(5 * second + 2, 3), :] = packed[2:5] + jnp.where(
+            low_lane[0:3], 0.0, tail
+        )
+        if second:
+            half_ref[core, 10:13, :] = jnp.where(
+                low_lane[0:3], before, pltpu.roll(packed, 2, 1)[5:8]
+            )
+        before = tail
         for half in range(2):
             low = f_ref[pl.ds(x * XROWS + 2 * half, 2), :]
             high = f_ref[pl.ds((x + 1) * XROWS - 4 + 2 * half, 2), :]
-            out_ref[pl.ds(32 + 8 * half + 2 * x, 2), :] = jnp.where(
+            half_ref[core, pl.ds(13 + 4 * half + 2 * second, 2), :] = jnp.where(
                 x2[half : half + 1] < 0, low, high
             )
+        if second:
+            for to in range(core, send_ref.shape[0] // SHARE, 2):
+                send_ref[pl.ds(SHARE * to, SHARE), :] = half_ref[core, 0:SHARE, :]
 
 
 def cell_quantities(sums):
-    low_lane = (lax.broadcasted_iota(jnp.int32, (DEPTH, LANES), 1) & 2) == 0
+    low_lane = (lax.broadcasted_iota(jnp.int32, (2, LANES), 1) & 2) == 0
     low, high = [], []
     for m in range(8):
-        own = sums[DEPTH * m : DEPTH * (m + 1)] * WEIGHT
-        other = jnp.where(low_lane, pltpu.roll(own, LANES - 2, 1), pltpu.roll(own, 2, 1))
-        low.append(jnp.where(low_lane, own, other))
-        high.append(jnp.where(low_lane, other, own))
+        if m < 5:
+            own = jnp.concatenate([sums[m : m + 1], sums[5 + m : 6 + m]], axis=0)
+            own = own * WEIGHT
+            other = jnp.where(
+                low_lane, pltpu.roll(own, LANES - 2, 1), pltpu.roll(own, 2, 1)
+            )
+            low.append(jnp.where(low_lane, own, other))
+            high.append(jnp.where(low_lane, other, own))
+        else:
+            own = jnp.broadcast_to(sums[5 + m : 6 + m], (2, LANES)) * WEIGHT
+            first = jnp.where(low_lane, own, pltpu.roll(own, 2, 1))
+            second = jnp.where(low_lane, pltpu.roll(own, LANES - 2, 1), own)
+            low.append(jnp.where(sublane((2, LANES)) == 0, first, second))
     n = low[0]
     inv = 1.0 / n
     u = [low[1 + k] * inv for k in range(3)]
@@ -144,7 +168,7 @@
     heat = []
     for k in range(3):
         cross = sum(u[j] * pressure[min(j, k), max(j, k)] for j in range(3))
-        heat.append(0.5 * (high[2 + k] + high[5 + k] - 2.0 * cross + u[k] * (2.0 * n * speed - energy)))
+        heat.append(0.5 * (high[2 + k] - 2.0 * cross + u[k] * (2.0 * n * speed - energy)))
     inv_t = 1.0 / temperature
     scale = (1.0 - diffusivity_ratio) / 5.0 * inv * inv_t * inv_t
     arg = 2.0 * math.pi * temperature
@@ -153,13 +177,46 @@
     return u + [h * scale for h in heat] + [inv_t, norm, rate]
 
 
-def blocks_kernel(copies, got_ref, f_ref, pattern_ref, slot_ref, send_ref, a_ref, h_ref):
-    sums = got_ref[0, 0:32, :]
-    for k in range(1, 16):
-        sums = sums + got_ref[k, 0:32, :]
+def cells_kernel(sources, got_ref, out_ref):
+    sums = got_ref[pl.ds(0, 16), :]
+    for k in range(1, sources):
+        sums = sums + got_ref[pl.ds(SHARE * k, 16), :]
     quantities = cell_quantities(sums)
-    filler = jnp.zeros((LANES - DEPTH * len(quantities), LANES), F32)
-    columns = jnp.concatenate(quantities + [filler], axis=0).T
+    filler = jnp.zeros((24 - 2 * len(quantities), LANES), F32)
+    table = jnp.concatenate(quantities + [filler], axis=0)
+    for k in range(3):
+        out_ref[k] = table[8 * k : 8 * k + 8]
+
+    upper = (sublane((8, LANES)) >> 2) & 1
+    even = lax.axis_index("vel") // 2 * 2
+    lanes, kept, rolled, values = [], [], [], []
+    for core in range(2):
+        at = SHARE * (even + core) + 21
+        first = jnp.broadcast_to(got_ref[pl.ds(at, 1), :], (8, LANES))
+        second = jnp.broadcast_to(got_ref[pl.ds(at + 1, 1), :], (8, LANES))
+        slot = jnp.where(upper == 0, first, second).astype(jnp.int32)
+        lanes.append(slot & (LANES - 1))
+        kept.append((slot >> 7) - upper)
+        rolled.append((slot >> 7) + upper)
+        values.append(jnp.zeros((8, LANES), F32))
+    for k in range(sources):
+        piece = got_ref[pl.ds(SHARE * k + 13, 8), :]
+        swapped = pltpu.roll(piece, 4, 0)
+        for core in range(2):
+            there = jnp.take_along_axis(piece, lanes[core], axis=1)
+            across = jnp.take_along_axis(swapped, lanes[core], axis=1)
+            value = jnp.where(kept[core] == 2 * k, there, values[core])
+            values[core] = jnp.where(rolled[core] == 2 * k + 1, across, value)
+    for core in range(2):
+        out_ref[3 + core] = values[core]
+
+
+def blocks_kernel(copies, got_ref, f_ref, pattern_ref, send_ref, a_ref, h_ref):
+    parts = [got_ref[half, k] for half in range(2) for k in range(3)]
+    filler = jnp.zeros((LANES - 48, LANES), F32)
+    columns = jnp.concatenate(parts + [filler], axis=0).T
+    core = lax.axis_index("vel") % 2
+    found = [got_ref[half, 3 + core] for half in range(2)]
 
     lane = lax.broadcasted_iota(jnp.int32, (8, LANES), 1)
     cell = (lane >> 3) & 7
@@ -167,24 +224,12 @@
     speed = stream_x * SPACING * ((lane & 7).astype(F32) + 0.5)
     chunk_gain = jnp.ones((8, LANES), F32)
     for x in range(DEPTH):
-        rate = jnp.broadcast_to(quantities[8][x : x + 1], (8, LANES))
+        rate = jnp.broadcast_to(parts[3 * (x // 2) + 2][x % 2 : x % 2 + 1], (8, LANES))
         rate = jnp.take_along_axis(rate, source, axis=1)
         chunk_gain = chunk_gain * (speed / (1.0 + speed + rate))
     for to in range(copies * CHUNKS):
         at = to % CHUNKS
         send_ref[pl.ds(CHUNK_ROWS * to + 16, 1), :] = chunk_gain[at : at + 1]
-
-    found = []
-    for half in range(2):
-        slot = slot_ref[half]
-        lane, group = slot & (LANES - 1), slot >> 7
-        value = jnp.zeros((8, LANES), F32)
-        for source in range(32):
-            piece = got_ref[source // 2, pl.ds(32 + 8 * (source % 2), 8), :]
-            value = jnp.where(
-                group == source, jnp.take_along_axis(piece, lane, axis=1), value
-            )
-        found.append(value)
 
     x1, x2, x3 = pattern_ref[0], pattern_ref[1], pattern_ref[2]
     ahead = x1 > 0
@@ -202,16 +247,16 @@
 
     ghosts = []
     for x in range(DEPTH):
-        four = jnp.concatenate(
-            [found[0][2 * x : 2 * x + 2], found[1][2 * x : 2 * x + 2]], axis=0
-        )
+        wall = found[x // 2]
+        at = 2 * (x % 2)
+        four = jnp.concatenate([wall[at : at + 2], wall[at + 4 : at + 6]], axis=0)
         ghosts.append(jnp.concatenate([four, four], axis=0))
 
     for i in range(XROWS // 8):
         a, b, target = [], [], []
         for x in range(DEPTH):
             def column(q):
-                at = DEPTH * q + x
+                at = 24 * (x // 2) + 2 * q + x % 2
                 return jnp.broadcast_to(
                     columns[8 * i : 8 * i + 8, at : at + 1], (8, LANES)
                 )
@@ -329,17 +374,18 @@
     mirror = mirror_slot.reshape(2, LANES)
     wall = wall_mask.transpose(1, 2, 0)
 
-    mine, kept, pattern, slots = pl.pallas_call(
+    sources = lax.axis_size("vel")
+    shares, kept, pattern = pl.pallas_call(
         moments_kernel,
         out_shape=[
-            pltpu.VMEM((48, LANES), F32),
+            pltpu.VMEM((sources * SHARE, LANES), F32),
             pltpu.VMEM((DEPTH * XROWS, LANES), F32),
             pltpu.VMEM((3 + 2 * DEPTH, 8, LANES), F32),
-            pltpu.VMEM((2, 8, LANES), jnp.int32),
         ],
         in_specs=[ANYWHERE] * 4,
-        out_specs=[ON_CHIP] * 4,
+        out_specs=[ON_CHIP] * 3,
         scratch_shapes=[
+            pltpu.VMEM((2, 24, LANES), F32),
             pltpu.VMEM((2, LANES), jnp.int32),
             pltpu.VMEM((2, LANES), jnp.int32),
             pltpu.VMEM((2, PLANES, DEPTH), jnp.int32),
@@ -347,7 +393,17 @@
             pltpu.SemaphoreType.DMA((3,)),
         ],
     )(f, point, mirror, wall)
-    everyone = lax.all_gather(mine, "vel")
+    partial = lax.all_to_all(
+        shares.reshape(sources, 1, SHARE * LANES), "vel", 0, 0, tiled=True
+    ).reshape(sources * SHARE, LANES)
+    cells = pl.pallas_call(
+        lambda *refs: cells_kernel(sources, *refs),
+        out_shape=pltpu.VMEM((5, 8, LANES), F32),
+        in_specs=[ON_CHIP],
+        out_specs=ON_CHIP,
+    )(held(partial))
+    pairs = [[k, k + 1] for k in range(0, sources, 2)]
+    everyone = lax.all_gather(cells, "vel", axis_index_groups=pairs)
     send, gains, holds = pl.pallas_call(
         lambda *refs: blocks_kernel(copies, *refs),
         out_shape=[
@@ -355,9 +411,9 @@
             pltpu.VMEM((DEPTH * XROWS, LANES), F32),
             pltpu.VMEM((DEPTH * XROWS, LANES), F32),
         ],
-        in_specs=[ON_CHIP] * 4,
+        in_specs=[ON_CHIP] * 3,
         out_specs=[ON_CHIP] * 3,
-    )(held(everyone), held(kept), held(pattern), held(slots))
+    )(held(everyone), held(kept), held(pattern))
     chain = lax.all_to_all(
         send.reshape(blocks, 1, CHUNK_ROWS * LANES), "space", 0, 0, tiled=True
     ).reshape(blocks * CHUNK_ROWS, LANES)

time: 57.6 us -> 57.9 us (level)
    all_gather x1, blocking collectives: 22 us -> 1.84 us  [shards(): everyone = lax.all_gather(cells, 'vel', axis_index_groups=pairs)]
    all_to_all x0 -> x1, blocking collectives: none -> 19.3 us  [shards(): lax.all_to_all(shares.reshape(sources, 1, SHARE * LANES), 'vel', 0, 0, ti...]
    all_to_all x1, blocking collectives: 22.8 us -> 23.6 us  [shards(): lax.all_to_all(send.reshape(blocks, 1, CHUNK_ROWS * LANES), 'space', 0, 0...]
    pallas_call x1 -> x2, Pallas kernels: 1.57 us -> 1.96 us  [the longest x1 1.72 us: shards(): pl.pallas_call(moments_kernel, out_shape=[pltpu.VMEM((sources * SHARE, LA...]
where the time goes in v5:
time: 57.9 us; the launch traced here: 57.2 us
  blocking collectives  53 us (92%)
  Pallas kernels  4.13 us (7%)
    all_to_all x1, blocking collectives, shards(): lax.all_to_all(send.reshape(blocks, 1, CHUNK_ROWS * LANES), 'space', 0, 0...  23.6 us
    all_to_all x1, blocking collectives, shards(): lax.all_to_all(shares.reshape(sources, 1, SHARE * LANES), 'vel', 0, 0, ti...  19.3 us
    all_to_all x1, blocking collectives, shards(): lax.all_to_all(enters, 'space', 0, 0, axis_index_groups=lines, tiled=True)  8.25 us
    all_gather x1, blocking collectives, shards(): everyone = lax.all_gather(cells, 'vel', axis_index_groups=pairs)  1.84 us
    pallas_call x1, Pallas kernels, shards(): pl.pallas_call(moments_kernel, out_shape=[pltpu.VMEM((sources * SHARE, LA...  1.72 us
    pallas_call x1, Pallas kernels, shards(): pl.pallas_call(lambda *refs: blocks_kernel(copies, *refs), out_shape=[plt...  1.18 us

profile of v5, /device:TPU:1, one launch (start us, length us, event | category | flops | bytes accessed | tf_op | source)
XLA Modules:
  0.0 57.2 jit_solution(15837669564006433228)
XLA Ops:
  0.0 1.7 %shard_map.46 = (f32[368,128]{1,0:T(8,128)S(1)}, f32[512,128]{1,0:T(8,128)S(1)}, f32[11,8,128]{2,1,0:T(8,128)S(1)}) custom-call(f32[512,128]{1,0:T(8,128)} %bitcast.25, s32[2,128]{1,0:T(2,128)} %bitcast.27, s32[2,128]{1,0:T(2,128)} %bitcast.28, s32[2,2,4]{2,1,0:T(2,128)} %bitcast.26), custom_call_target="tpu_custom_call" | custom-call | tf_op jit(solution)/shard_map/pallas_call | solution.py:378
  1.7 19.3 %all_to_all.15 = f32[16,1,2944]{2,1,0:T(1,128)S(1)} all-to-all(f32[16,1,2944]{2,1,0:T(1,128)S(1)} %bitcast.23), channel_id=1, replica_groups=mesh['space'=32,'vel'=16] {'vel'}, dimensions={0} | all-to-all | bytes 376832 | tf_op jit(solution)/shard_map/all_to_all | solution.py:396
  21.1 0.2 shard_map.47
  21.3 1.8 %all-gather = f32[10,8,128]{2,1,0:T(8,128)S(1)} all-gather(f32[5,8,128]{2,1,0:T(8,128)S(1)} %shard_map.47), channel_id=2, replica_groups={{0,1},{2,3},{4,5},{6,7},{8,9},{10,11},{12,13},{14,15},{16,17},{18,19},{..., dimensions={0}, use_global_device_ids=true | all-gather | bytes 61440 | tf_op jit(solution)/shard_map/all_gather | solution.py:406
  23.1 1.2 %shard_map.48 = (f32[544,128]{1,0:T(8,128)S(1)}, f32[512,128]{1,0:T(8,128)S(1)}, f32[512,128]{1,0:T(8,128)S(1)}) custom-call(f32[2,5,8,128]{3,2,1,0:T(8,128)S(1)} %bitcast.24, f32[512,128]{1,0:T(8,128)S(1)} %get-tuple-element.12.refs_1_, f32[11,8,128]{2,1,0:T(8,128)S(1)} %get-tuple-element.13.refs_2_.refs_1_.pattern_ref), custom_call_target="tpu_custom_call" | custom-call | tf_op jit(solution)/shard_map/pallas_call | solution.py:407
  24.3 23.6 %all_to_all.16 = f32[32,1,2176]{2,1,0:T(1,128)S(1)} all-to-all(f32[32,1,2176]{2,1,0:T(1,128)S(1)} %bitcast.21), channel_id=1, replica_groups=mesh['space'=32,'vel'=16] {'space'}, dimensions={0} | all-to-all | bytes 557056 | tf_op jit(solution)/shard_map/all_to_all | solution.py:417
  47.9 0.2 shard_map.49
  48.2 8.3 %all_to_all.17 = f32[8,16,128]{2,1,0:T(8,128)S(1)} all-to-all(f32[8,16,128]{2,1,0:T(8,128)S(1)} %shard_map.49), channel_id=1, replica_groups={{0,16,32,48,64,80,96,112},{128,144,160,176,192,208,224,240},{256,272,28..., dimensions={0} | all-to-all | bytes 131072 | tf_op jit(solution)/shard_map/all_to_all | solution.py:431
  56.4 0.8 %shard_map.50 = f32[512,128]{1,0:T(8,128)} custom-call(f32[128,128]{1,0:T(8,128)S(1)} %bitcast.22, f32[512,128]{1,0:T(8,128)S(1)} %get-tuple-element.15.a_ref, f32[512,128]{1,0:T(8,128)S(1)} %get-tuple-element.16.h_ref, f32[11,8,128]{2,1,0:T(8,128)S(1)} %get-tuple-element.13.refs_2_.refs_1_.pattern_ref), custom_call_target="tpu_custom_call" | custom-call | tf_op jit(solution)/shard_map/pallas_call | solution.py:432

commit v6 on v4

--- a/solution.py
+++ b/solution.py
@@ -48,7 +48,7 @@
 
 def moments_kernel(
     f_hbm, point_hbm, mirror_hbm, wall_hbm,
-    out_ref, f_ref, pattern_ref, slot_ref,
+    out_ref, f_ref, pattern_ref, slot_ref, weight_ref,
     point_ref, mirror_ref, wall_ref, f_sem, small_sem,
 ):
     small = [
@@ -79,6 +79,17 @@
             x1 * x3, x2 * x3, *coarse,
             *[c - r for c, r in zip(cubes, coarse)],
         ]
+    weights = []
+    for half in range(2):
+        x1, x2, x3 = velocity(points[half : half + 1])
+        square = x1 * x1 + x2 * x2 + x3 * x3
+        coarse = square.astype(BF16).astype(F32)
+        one, zero = jnp.ones_like(x1), jnp.zeros_like(x1)
+        left = [one, x1, x2, x3, coarse, square - coarse] + [zero] * 10
+        right = [zero] * 6 + [one, x1, x2, x3] + [zero] * 6
+        weights += [jnp.concatenate(pair, axis=1) for pair in zip(left, right)]
+    weights = jnp.concatenate(weights, axis=0).astype(BF16)
+    weight_ref[...] = jnp.concatenate([weights] * 3 + [jnp.zeros_like(weights)], axis=0)
     table = jnp.concatenate(tables, axis=0).astype(BF16)
     table = jnp.concatenate([table] * 3, axis=1)
     low_lane = (lax.broadcasted_iota(jnp.int32, (8, LANES), 1) & 2) == 0
@@ -149,17 +160,47 @@
     scale = (1.0 - diffusivity_ratio) / 5.0 * inv * inv_t * inv_t
     arg = 2.0 * math.pi * temperature
     norm = n / (arg * jnp.sqrt(arg))
+    heat = [h * scale for h in heat]
     rate = relaxation_multiplier * n * jnp.exp((1.0 - shear_power_index) * jnp.log(temperature))
-    return u + [h * scale for h in heat] + [inv_t, norm, rate]
-
-
-def blocks_kernel(copies, got_ref, f_ref, pattern_ref, slot_ref, send_ref, a_ref, h_ref):
+    ratio = [speed * inv_t] + [-2.0 * v * inv_t for v in u] + [inv_t]
+    along = [-(u[0] * heat[0] + u[1] * heat[1] + u[2] * heat[2])] + heat
+    return ratio + along, norm, rate
+
+
+def blocks_kernel(
+    copies, got_ref, f_ref, pattern_ref, slot_ref, weight_ref, send_ref, a_ref, h_ref, poly_ref
+):
     sums = got_ref[0, 0:32, :]
     for k in range(1, 16):
         sums = sums + got_ref[k, 0:32, :]
-    quantities = cell_quantities(sums)
-    filler = jnp.zeros((LANES - DEPTH * len(quantities), LANES), F32)
-    columns = jnp.concatenate(quantities + [filler], axis=0).T
+    coefficients, norm, rates = cell_quantities(sums)
+    parts = [[], [], []]
+    for c in coefficients:
+        for part in parts:
+            piece = c.astype(BF16).astype(F32)
+            part.append(piece)
+            c = c - piece
+    rows = parts[0] + parts[1] + parts[2] + [norm, rates]
+    filler = jnp.zeros((LANES - DEPTH * len(rows), LANES), F32)
+    columns = jnp.concatenate(rows + [filler], axis=0).T
+
+    lane = lax.broadcasted_iota(jnp.int32, (8, LANES), 1)
+    term = lane & 15
+    term = jnp.where(term > 9, 0, jnp.where(term > 4, term - 1, term))
+    part = jnp.where(lane < 96, lane >> 5, 0)
+    source = DEPTH * (len(coefficients) * part + term)
+    same = ((sublane((8, LANES)) >> 1) & 1) == ((lane >> 4) & 1)
+    left = []
+    for x in range(DEPTH):
+        for i in range(XROWS // 8):
+            value = jnp.take_along_axis(columns[8 * i : 8 * i + 8], source + x, axis=1)
+            left.append(jnp.where(same, value, 0.0))
+    poly_ref[...] = lax.dot_general(
+        jnp.concatenate(left, axis=0).astype(BF16),
+        weight_ref[...],
+        (((1,), (0,)), ((), ())),
+        preferred_element_type=F32,
+    )
 
     lane = lax.broadcasted_iota(jnp.int32, (8, LANES), 1)
     cell = (lane >> 3) & 7
@@ -167,7 +208,7 @@
     speed = stream_x * SPACING * ((lane & 7).astype(F32) + 0.5)
     chunk_gain = jnp.ones((8, LANES), F32)
     for x in range(DEPTH):
-        rate = jnp.broadcast_to(quantities[8][x : x + 1], (8, LANES))
+        rate = jnp.broadcast_to(rates[x : x + 1], (8, LANES))
         rate = jnp.take_along_axis(rate, source, axis=1)
         chunk_gain = chunk_gain * (speed / (1.0 + speed + rate))
     for to in range(copies * CHUNKS):
@@ -211,19 +252,17 @@
         a, b, target = [], [], []
         for x in range(DEPTH):
             def column(q):
-                at = DEPTH * q + x
+                at = DEPTH * (3 * len(coefficients) + q) + x
                 return jnp.broadcast_to(
                     columns[8 * i : 8 * i + 8, at : at + 1], (8, LANES)
                 )
 
             base = x * XROWS + 8 * i
             f = f_ref[pl.ds(base, 8), :]
-            c1, c2, c3 = x1 - column(0), x2 - column(1), x3 - column(2)
-            square = c1 * c1 + c2 * c2 + c3 * c3
-            along = c1 * column(3) + c2 * column(4) + c3 * column(5)
-            ratio = square * column(6)
-            shakhov = column(7) * jnp.exp(-0.5 * ratio) * (1.0 + along * (ratio - 5.0))
-            rate = column(8)
+            ratio = poly_ref[pl.ds(base, 8), 0:LANES]
+            along = poly_ref[pl.ds(base, 8), LANES : 2 * LANES]
+            shakhov = column(0) * jnp.exp(-0.5 * ratio) * (1.0 + along * (ratio - 5.0))
+            rate = column(1)
 
             def ghost(wall):
                 mask = pattern_ref[3 + 2 * x + wall]
@@ -329,16 +368,17 @@
     mirror = mirror_slot.reshape(2, LANES)
     wall = wall_mask.transpose(1, 2, 0)
 
-    mine, kept, pattern, slots = pl.pallas_call(
+    mine, kept, pattern, slots, weights = pl.pallas_call(
         moments_kernel,
         out_shape=[
             pltpu.VMEM((48, LANES), F32),
             pltpu.VMEM((DEPTH * XROWS, LANES), F32),
             pltpu.VMEM((3 + 2 * DEPTH, 8, LANES), F32),
             pltpu.VMEM((2, 8, LANES), jnp.int32),
+            pltpu.VMEM((LANES, 2 * LANES), BF16),
         ],
         in_specs=[ANYWHERE] * 4,
-        out_specs=[ON_CHIP] * 4,
+        out_specs=[ON_CHIP] * 5,
         scratch_shapes=[
             pltpu.VMEM((2, LANES), jnp.int32),
             pltpu.VMEM((2, LANES), jnp.int32),
@@ -355,9 +395,10 @@
             pltpu.VMEM((DEPTH * XROWS, LANES), F32),
             pltpu.VMEM((DEPTH * XROWS, LANES), F32),
         ],
-        in_specs=[ON_CHIP] * 4,
+        in_specs=[ON_CHIP] * 5,
         out_specs=[ON_CHIP] * 3,
-    )(held(everyone), held(kept), held(pattern), held(slots))
+        scratch_shapes=[pltpu.VMEM((DEPTH * XROWS, 2 * LANES), F32)],
+    )(held(everyone), held(kept), held(pattern), held(slots), held(weights))
     chain = lax.all_to_all(
         send.reshape(blocks, 1, CHUNK_ROWS * LANES), "space", 0, 0, tiled=True
     ).reshape(blocks * CHUNK_ROWS, LANES)

time: 57.6 us -> 57 us (0.990)
  no operation moved by 1% of the time
where the time goes in v6:
time: 57 us; the launch traced here: 56.3 us
  blocking collectives  53 us (93%)
  Pallas kernels  3.31 us (6%)
    all_to_all x1, blocking collectives, shards(): lax.all_to_all(send.reshape(blocks, 1, CHUNK_ROWS * LANES), 'space', 0, 0...  22.8 us
    all_gather x1, blocking collectives, shards(): everyone = lax.all_gather(mine, 'vel')  22 us
    all_to_all x1, blocking collectives, shards(): lax.all_to_all(enters, 'space', 0, 0, axis_index_groups=lines, tiled=True)  8.25 us
    pallas_call x1, Pallas kernels, shards(): pl.pallas_call(moments_kernel, out_shape=[pltpu.VMEM((48, LANES), F32), p...  1.57 us

profile of v6, /device:TPU:1, one launch (start us, length us, event | category | flops | bytes accessed | tf_op | source)
XLA Modules:
  0.0 56.3 jit_solution(11688999669311049970)
XLA Ops:
  0.0 1.6 %shard_map.46 = (f32[48,128]{1,0:T(8,128)S(1)}, f32[512,128]{1,0:T(8,128)S(1)}, f32[11,8,128]{2,1,0:T(8,128)S(1)}, s32[2,8,128]{2,1,0:T(8,128)S(1)}, bf16[128,256]{1,0:T(8,128)(2,1)S(1)}) custom-call(f32[512,128]{1,0:T(8,128)} %bitcast.21, s32[2,128]{1,0:T(2,128)} %bitcast.23, s32[2,128]{1,0:T(2,128)} %bitcast.24, s32[2,2,4]{2,1,0:T(2,128)} %bitcast.22), custom_call_target="tpu_custom_call" | custom-call | tf_op jit(solution)/shard_map/pallas_call | solution.py:371
  1.6 22.0 %all-gather = f32[768,128]{1,0:T(8,128)S(1)} all-gather(f32[48,128]{1,0:T(8,128)S(1)} %get-tuple-element.13), channel_id=2, replica_groups=mesh['space'=32,'vel'=16] {'vel'}, dimensions={0}, use_global_device_ids=true | all-gather | bytes 417792 | tf_op jit(solution)/shard_map/all_gather | solution.py:390
  23.5 0.8 %shard_map.47 = (f32[544,128]{1,0:T(8,128)S(1)}, f32[512,128]{1,0:T(8,128)S(1)}, f32[512,128]{1,0:T(8,128)S(1)}) custom-call(f32[16,48,128]{2,1,0:T(8,128)S(1)} %bitcast.17, f32[512,128]{1,0:T(8,128)S(1)} %get-tuple-element.14.refs_1_, f32[11,8,128]{2,1,0:T(8,128)S(1)} %get-tuple-element.15.refs_2_.refs_1_.pattern_ref, ...), custom_call_target="tpu_custom_call" | custom-call | tf_op jit(solution)/shard_map/pallas_call | solution.py:391
  24.3 22.8 %all_to_all.10 = f32[32,1,2176]{2,1,0:T(1,128)S(1)} all-to-all(f32[32,1,2176]{2,1,0:T(1,128)S(1)} %bitcast.19), channel_id=1, replica_groups=mesh['space'=32,'vel'=16] {'space'}, dimensions={0} | all-to-all | bytes 557056 | tf_op jit(solution)/shard_map/all_to_all | solution.py:402
  47.1 0.2 shard_map.48
  47.3 8.3 %all_to_all.11 = f32[8,16,128]{2,1,0:T(8,128)S(1)} all-to-all(f32[8,16,128]{2,1,0:T(8,128)S(1)} %shard_map.48), channel_id=1, replica_groups={{0,16,32,48,64,80,96,112},{128,144,160,176,192,208,224,240},{256,272,28..., dimensions={0} | all-to-all | bytes 131072 | tf_op jit(solution)/shard_map/all_to_all | solution.py:416
  55.6 0.8 %shard_map.49 = f32[512,128]{1,0:T(8,128)} custom-call(f32[128,128]{1,0:T(8,128)S(1)} %bitcast.20, f32[512,128]{1,0:T(8,128)S(1)} %get-tuple-element.19.a_ref, f32[512,128]{1,0:T(8,128)S(1)} %get-tuple-element.20.h_ref, f32[11,8,128]{2,1,0:T(8,128)S(1)} %get-tuple-element.15.refs_2_.refs_1_.pattern_ref), custom_call_target="tpu_custom_call" | custom-call | tf_op jit(solution)/shard_map/pallas_call | solution.py:417

commit v7 on v6

--- a/solution.py
+++ b/solution.py
@@ -27,6 +27,9 @@
 
 CHUNKS = 8
 CHUNK_ROWS = 17
+
+ORDER = list(range(31, -1, -1))
+LINE = [7, 6, 5, 4, 3, 2, 1, 0]
 
 
 def velocity(points):
@@ -213,7 +216,7 @@
         chunk_gain = chunk_gain * (speed / (1.0 + speed + rate))
     for to in range(copies * CHUNKS):
         at = to % CHUNKS
-        send_ref[pl.ds(CHUNK_ROWS * to + 16, 1), :] = chunk_gain[at : at + 1]
+        send_ref[pl.ds(CHUNK_ROWS * ORDER.index(to) + 16, 1), :] = chunk_gain[at : at + 1]
 
     found = []
     for half in range(2):
@@ -298,7 +301,7 @@
             h_ref[pl.ds(t * XROWS + 8 * i, 8), :] = hold
         for copy in range(copies):
             to = copy * CHUNKS + i // 2
-            send_ref[pl.ds(CHUNK_ROWS * to + 8 * (i % 2), 8), :] = hold
+            send_ref[pl.ds(CHUNK_ROWS * ORDER.index(to) + 8 * (i % 2), 8), :] = hold
 
 
 def chain_kernel(copies, got_ref, pattern_ref, out_ref, gain_ref, keep_ref):
@@ -310,7 +313,7 @@
         cell = 2 * (2 * half + (row >> 2)) + (row & 1)
         source = 8 * cell + which
         for k in range(blocks):
-            gain = jnp.broadcast_to(got_ref[pl.ds(CHUNK_ROWS * k + 16, 1), :], (8, LANES))
+            gain = jnp.broadcast_to(got_ref[pl.ds(CHUNK_ROWS * ORDER.index(k) + 16, 1), :], (8, LANES))
             gain_ref[k] = jnp.take_along_axis(gain, source, axis=1)
         enter = jnp.zeros((8, LANES), F32)
         for k in range(blocks):
@@ -319,14 +322,14 @@
             gain = jnp.where(ahead, gain_ref[k], gain_ref[back])
             hold = jnp.where(
                 ahead,
-                got_ref[pl.ds(CHUNK_ROWS * k + 8 * half, 8), :],
-                got_ref[pl.ds(CHUNK_ROWS * back + 8 * half, 8), :],
+                got_ref[pl.ds(CHUNK_ROWS * ORDER.index(k) + 8 * half, 8), :],
+                got_ref[pl.ds(CHUNK_ROWS * ORDER.index(back) + 8 * half, 8), :],
             )
             enter = gain * enter + hold
     first = lax.axis_index("space") // CHUNKS * CHUNKS
     for half in range(2):
         for x in range(CHUNKS):
-            out_ref[x, pl.ds(8 * half, 8), :] = jnp.where(
+            out_ref[LINE.index(x), pl.ds(8 * half, 8), :] = jnp.where(
                 ahead, keep_ref[half, first + x], keep_ref[half, blocks - 1 - x - first]
             )
 
@@ -336,7 +339,7 @@
     copies = []
     for x, mate in ((0, DEPTH - 1), (1, DEPTH - 2)):
         for i in range(XROWS // 8):
-            enter = enter_ref[pl.ds(8 * i, 8), :]
+            enter = enter_ref[pl.ds(16 * LINE.index(i // 2) + 8 * (i % 2), 8), :]
             value = []
             for t in (x, mate):
                 at = pl.ds(t * XROWS + 8 * i, 8)
@@ -400,7 +403,7 @@
         scratch_shapes=[pltpu.VMEM((DEPTH * XROWS, 2 * LANES), F32)],
     )(held(everyone), held(kept), held(pattern), held(slots), held(weights))
     chain = lax.all_to_all(
-        send.reshape(blocks, 1, CHUNK_ROWS * LANES), "space", 0, 0, tiled=True
+        send.reshape(blocks, 1, CHUNK_ROWS * LANES), "space", 0, 0, axis_index_groups=[ORDER], tiled=True
     ).reshape(blocks * CHUNK_ROWS, LANES)
     enters = pl.pallas_call(
         lambda *refs: chain_kernel(copies, *refs),
@@ -412,7 +415,7 @@
             pltpu.VMEM((2, blocks, 8, LANES), F32),
         ],
     )(held(chain), held(pattern))
-    lines = [[CHUNKS * z + x for x in range(CHUNKS)] for z in range(copies)]
+    lines = [[CHUNKS * z + x for x in LINE] for z in range(copies)]
     enter = lax.all_to_all(enters, "space", 0, 0, axis_index_groups=lines, tiled=True)
     out = pl.pallas_call(
         finish_kernel,

time: 57 us -> 54.1 us (0.949)
  blocking collectives: 53 us -> 50.6 us
    all_to_all x1, blocking collectives: 22.8 us -> 20.3 us  [shards(): lax.all_to_all(send.reshape(blocks, 1, CHUNK_ROWS * LANES), 'space', 0, 0...]
where the time goes in v7:
time: 54.1 us; the launch traced here: 53.9 us
  blocking collectives  50.6 us (94%)
  Pallas kernels  3.31 us (6%)
    all_gather x1, blocking collectives, shards(): everyone = lax.all_gather(mine, 'vel')  22 us
    all_to_all x1, blocking collectives, shards(): lax.all_to_all(send.reshape(blocks, 1, CHUNK_ROWS * LANES), 'space', 0, 0...  20.3 us
    all_to_all x1, blocking collectives, shards(): lax.all_to_all(enters, 'space', 0, 0, axis_index_groups=lines, tiled=True)  8.4 us
    pallas_call x1, Pallas kernels, shards(): pl.pallas_call(moments_kernel, out_shape=[pltpu.VMEM((48, LANES), F32), p...  1.57 us

profile of v7, /device:TPU:1, one launch (start us, length us, event | category | flops | bytes accessed | tf_op | source)
XLA Modules:
  0.0 53.9 jit_solution(3744678666029099200)
XLA Ops:
  0.0 1.6 %shard_map.46 = (f32[48,128]{1,0:T(8,128)S(1)}, f32[512,128]{1,0:T(8,128)S(1)}, f32[11,8,128]{2,1,0:T(8,128)S(1)}, s32[2,8,128]{2,1,0:T(8,128)S(1)}, bf16[128,256]{1,0:T(8,128)(2,1)S(1)}) custom-call(f32[512,128]{1,0:T(8,128)} %bitcast.21, s32[2,128]{1,0:T(2,128)} %bitcast.23, s32[2,128]{1,0:T(2,128)} %bitcast.24, s32[2,2,4]{2,1,0:T(2,128)} %bitcast.22), custom_call_target="tpu_custom_call" | custom-call | tf_op jit(solution)/shard_map/pallas_call | solution.py:374
  1.6 22.0 %all-gather = f32[768,128]{1,0:T(8,128)S(1)} all-gather(f32[48,128]{1,0:T(8,128)S(1)} %get-tuple-element.13), channel_id=2, replica_groups=mesh['space'=32,'vel'=16] {'vel'}, dimensions={0}, use_global_device_ids=true | all-gather | bytes 417792 | tf_op jit(solution)/shard_map/all_gather | solution.py:393
  23.5 0.8 %shard_map.47 = (f32[544,128]{1,0:T(8,128)S(1)}, f32[512,128]{1,0:T(8,128)S(1)}, f32[512,128]{1,0:T(8,128)S(1)}) custom-call(f32[16,48,128]{2,1,0:T(8,128)S(1)} %bitcast.17, f32[512,128]{1,0:T(8,128)S(1)} %get-tuple-element.14.refs_1_, f32[11,8,128]{2,1,0:T(8,128)S(1)} %get-tuple-element.15.refs_2_.refs_1_.pattern_ref, ...), custom_call_target="tpu_custom_call" | custom-call | tf_op jit(solution)/shard_map/pallas_call | solution.py:394
  24.3 20.3 %all_to_all.10 = f32[32,1,2176]{2,1,0:T(1,128)S(1)} all-to-all(f32[32,1,2176]{2,1,0:T(1,128)S(1)} %bitcast.19), channel_id=1, replica_groups={{496,480,464,448,432,416,400,384,368,352,336,320,304,288,272,256,240,22..., dimensions={0} | all-to-all | bytes 557056 | tf_op jit(solution)/shard_map/all_to_all | solution.py:405
  44.5 0.2 shard_map.48
  44.8 8.4 %all_to_all.11 = f32[8,16,128]{2,1,0:T(8,128)S(1)} all-to-all(f32[8,16,128]{2,1,0:T(8,128)S(1)} %shard_map.48), channel_id=1, replica_groups={{112,96,80,64,48,32,16,0},{240,224,208,192,176,160,144,128},{368,352,33..., dimensions={0} | all-to-all | bytes 131072 | tf_op jit(solution)/shard_map/all_to_all | solution.py:419
  53.2 0.7 %shard_map.49 = f32[512,128]{1,0:T(8,128)} custom-call(f32[128,128]{1,0:T(8,128)S(1)} %bitcast.20, f32[512,128]{1,0:T(8,128)S(1)} %get-tuple-element.19.a_ref, f32[512,128]{1,0:T(8,128)S(1)} %get-tuple-element.20.h_ref, f32[11,8,128]{2,1,0:T(8,128)S(1)} %get-tuple-element.15.refs_2_.refs_1_.pattern_ref), custom_call_target="tpu_custom_call" | custom-call | tf_op jit(solution)/shard_map/pallas_call | solution.py:420

commit v8 on v5

--- a/solution.py
+++ b/solution.py
@@ -28,6 +28,9 @@
 CHUNKS = 8
 CHUNK_ROWS = 17
 
+ORDER = list(range(31, -1, -1))
+LINE = [7, 6, 5, 4, 3, 2, 1, 0]
+
 SHARE = 23
 
 
@@ -50,7 +53,7 @@
 
 def moments_kernel(
     f_hbm, point_hbm, mirror_hbm, wall_hbm,
-    send_ref, f_ref, pattern_ref,
+    send_ref, f_ref, pattern_ref, weight_ref,
     half_ref, point_ref, mirror_ref, wall_ref, f_sem, small_sem,
 ):
     small = [
@@ -81,6 +84,17 @@
             x1 * x3, x2 * x3, *coarse,
             *[c - r for c, r in zip(cubes, coarse)],
         ]
+    weights = []
+    for half in range(2):
+        x1, x2, x3 = velocity(points[half : half + 1])
+        square = x1 * x1 + x2 * x2 + x3 * x3
+        coarse = square.astype(BF16).astype(F32)
+        one, zero = jnp.ones_like(x1), jnp.zeros_like(x1)
+        left = [one, x1, x2, x3, coarse, square - coarse] + [zero] * 10
+        right = [zero] * 6 + [one, x1, x2, x3] + [zero] * 6
+        weights += [jnp.concatenate(pair, axis=1) for pair in zip(left, right)]
+    weights = jnp.concatenate(weights, axis=0).astype(BF16)
+    weight_ref[...] = jnp.concatenate([weights] * 3 + [jnp.zeros_like(weights)], axis=0)
     table = jnp.concatenate(tables, axis=0).astype(BF16)
     table = jnp.concatenate([table] * 3, axis=1)
     low_lane = (lax.broadcasted_iota(jnp.int32, (8, LANES), 1) & 2) == 0
@@ -136,7 +150,7 @@
                 x2[half : half + 1] < 0, low, high
             )
         if second:
-            for to in range(core, send_ref.shape[0] // SHARE, 2):
+            for to in range(1 - core, send_ref.shape[0] // SHARE, 2):
                 send_ref[pl.ds(SHARE * to, SHARE), :] = half_ref[core, 0:SHARE, :]
 
 
@@ -173,8 +187,11 @@
     scale = (1.0 - diffusivity_ratio) / 5.0 * inv * inv_t * inv_t
     arg = 2.0 * math.pi * temperature
     norm = n / (arg * jnp.sqrt(arg))
+    heat = [h * scale for h in heat]
     rate = relaxation_multiplier * n * jnp.exp((1.0 - shear_power_index) * jnp.log(temperature))
-    return u + [h * scale for h in heat] + [inv_t, norm, rate]
+    ratio = [speed * inv_t] + [-2.0 * v * inv_t for v in u] + [inv_t]
+    along = [-(u[0] * heat[0] + u[1] * heat[1] + u[2] * heat[2])] + heat
+    return ratio + along + [norm, rate]
 
 
 def cells_kernel(sources, got_ref, out_ref):
@@ -188,10 +205,10 @@
         out_ref[k] = table[8 * k : 8 * k + 8]
 
     upper = (sublane((8, LANES)) >> 2) & 1
-    even = lax.axis_index("vel") // 2 * 2
+    even = sources - 1 - lax.axis_index("vel") // 2 * 2
     lanes, kept, rolled, values = [], [], [], []
     for core in range(2):
-        at = SHARE * (even + core) + 21
+        at = SHARE * (even - core) + 21
         first = jnp.broadcast_to(got_ref[pl.ds(at, 1), :], (8, LANES))
         second = jnp.broadcast_to(got_ref[pl.ds(at + 1, 1), :], (8, LANES))
         slot = jnp.where(upper == 0, first, second).astype(jnp.int32)
@@ -202,19 +219,49 @@
     for k in range(sources):
         piece = got_ref[pl.ds(SHARE * k + 13, 8), :]
         swapped = pltpu.roll(piece, 4, 0)
+        owner = sources - 1 - k
         for core in range(2):
             there = jnp.take_along_axis(piece, lanes[core], axis=1)
             across = jnp.take_along_axis(swapped, lanes[core], axis=1)
-            value = jnp.where(kept[core] == 2 * k, there, values[core])
-            values[core] = jnp.where(rolled[core] == 2 * k + 1, across, value)
+            value = jnp.where(kept[core] == 2 * owner, there, values[core])
+            values[core] = jnp.where(rolled[core] == 2 * owner + 1, across, value)
     for core in range(2):
         out_ref[3 + core] = values[core]
 
 
-def blocks_kernel(copies, got_ref, f_ref, pattern_ref, send_ref, a_ref, h_ref):
-    parts = [got_ref[half, k] for half in range(2) for k in range(3)]
-    filler = jnp.zeros((LANES - 48, LANES), F32)
-    columns = jnp.concatenate(parts + [filler], axis=0).T
+def blocks_kernel(
+    copies, got_ref, f_ref, pattern_ref, weight_ref, send_ref, a_ref, h_ref, poly_ref
+):
+    halves = [
+        jnp.concatenate([got_ref[half, k] for k in range(3)], axis=0) for half in range(2)
+    ]
+    rates = [halves[x // 2][20 + x % 2 : 21 + x % 2] for x in range(DEPTH)]
+    rows, left = [], halves
+    for part in range(3):
+        pieces = [h.astype(BF16).astype(F32) for h in left]
+        rows += [p[0:18] for p in pieces]
+        left = [h - p for h, p in zip(left, pieces)]
+    rows += [h[18:22] for h in halves]
+    filler = jnp.zeros((LANES - 116, LANES), F32)
+    columns = jnp.concatenate(rows + [filler], axis=0).T
+
+    lane = lax.broadcasted_iota(jnp.int32, (8, LANES), 1)
+    term = lane & 15
+    term = jnp.where(term > 9, 0, jnp.where(term > 4, term - 1, term))
+    source = 36 * jnp.where(lane < 96, lane >> 5, 0) + 2 * term
+    same = ((sublane((8, LANES)) >> 1) & 1) == ((lane >> 4) & 1)
+    left = []
+    for x in range(DEPTH):
+        at = source + (18 * (x // 2) + x % 2)
+        for i in range(XROWS // 8):
+            value = jnp.take_along_axis(columns[8 * i : 8 * i + 8], at, axis=1)
+            left.append(jnp.where(same, value, 0.0))
+    poly_ref[...] = lax.dot_general(
+        jnp.concatenate(left, axis=0).astype(BF16),
+        weight_ref[...],
+        (((1,), (0,)), ((), ())),
+        preferred_element_type=F32,
+    )
     core = lax.axis_index("vel") % 2
     found = [got_ref[half, 3 + core] for half in range(2)]
 
@@ -224,12 +271,12 @@
     speed = stream_x * SPACING * ((lane & 7).astype(F32) + 0.5)
     chunk_gain = jnp.ones((8, LANES), F32)
     for x in range(DEPTH):
-        rate = jnp.broadcast_to(parts[3 * (x // 2) + 2][x % 2 : x % 2 + 1], (8, LANES))
+        rate = jnp.broadcast_to(rates[x], (8, LANES))
         rate = jnp.take_along_axis(rate, source, axis=1)
         chunk_gain = chunk_gain * (speed / (1.0 + speed + rate))
     for to in range(copies * CHUNKS):
         at = to % CHUNKS
-        send_ref[pl.ds(CHUNK_ROWS * to + 16, 1), :] = chunk_gain[at : at + 1]
+        send_ref[pl.ds(CHUNK_ROWS * ORDER.index(to) + 16, 1), :] = chunk_gain[at : at + 1]
 
     x1, x2, x3 = pattern_ref[0], pattern_ref[1], pattern_ref[2]
     ahead = x1 > 0
@@ -256,19 +303,17 @@
         a, b, target = [], [], []
         for x in range(DEPTH):
             def column(q):
-                at = 24 * (x // 2) + 2 * q + x % 2
+                at = 108 + 4 * (x // 2) + 2 * q + x % 2
                 return jnp.broadcast_to(
                     columns[8 * i : 8 * i + 8, at : at + 1], (8, LANES)
                 )
 
             base = x * XROWS + 8 * i
             f = f_ref[pl.ds(base, 8), :]
-            c1, c2, c3 = x1 - column(0), x2 - column(1), x3 - column(2)
-            square = c1 * c1 + c2 * c2 + c3 * c3
-            along = c1 * column(3) + c2 * column(4) + c3 * column(5)
-            ratio = square * column(6)
-            shakhov = column(7) * jnp.exp(-0.5 * ratio) * (1.0 + along * (ratio - 5.0))
-            rate = column(8)
+            ratio = poly_ref[pl.ds(base, 8), 0:LANES]
+            along = poly_ref[pl.ds(base, 8), LANES : 2 * LANES]
+            shakhov = column(0) * jnp.exp(-0.5 * ratio) * (1.0 + along * (ratio - 5.0))
+            rate = column(1)
 
             def ghost(wall):
                 mask = pattern_ref[3 + 2 * x + wall]
@@ -304,7 +349,7 @@
             h_ref[pl.ds(t * XROWS + 8 * i, 8), :] = hold
         for copy in range(copies):
             to = copy * CHUNKS + i // 2
-            send_ref[pl.ds(CHUNK_ROWS * to + 8 * (i % 2), 8), :] = hold
+            send_ref[pl.ds(CHUNK_ROWS * ORDER.index(to) + 8 * (i % 2), 8), :] = hold
 
 
 def chain_kernel(copies, got_ref, pattern_ref, out_ref, gain_ref, keep_ref):
@@ -316,7 +361,7 @@
         cell = 2 * (2 * half + (row >> 2)) + (row & 1)
         source = 8 * cell + which
         for k in range(blocks):
-            gain = jnp.broadcast_to(got_ref[pl.ds(CHUNK_ROWS * k + 16, 1), :], (8, LANES))
+            gain = jnp.broadcast_to(got_ref[pl.ds(CHUNK_ROWS * ORDER.index(k) + 16, 1), :], (8, LANES))
             gain_ref[k] = jnp.take_along_axis(gain, source, axis=1)
         enter = jnp.zeros((8, LANES), F32)
         for k in range(blocks):
@@ -325,14 +370,14 @@
             gain = jnp.where(ahead, gain_ref[k], gain_ref[back])
             hold = jnp.where(
                 ahead,
-                got_ref[pl.ds(CHUNK_ROWS * k + 8 * half, 8), :],
-                got_ref[pl.ds(CHUNK_ROWS * back + 8 * half, 8), :],
+                got_ref[pl.ds(CHUNK_ROWS * ORDER.index(k) + 8 * half, 8), :],
+                got_ref[pl.ds(CHUNK_ROWS * ORDER.index(back) + 8 * half, 8), :],
             )
             enter = gain * enter + hold
     first = lax.axis_index("space") // CHUNKS * CHUNKS
     for half in range(2):
         for x in range(CHUNKS):
-            out_ref[x, pl.ds(8 * half, 8), :] = jnp.where(
+            out_ref[LINE.index(x), pl.ds(8 * half, 8), :] = jnp.where(
                 ahead, keep_ref[half, first + x], keep_ref[half, blocks - 1 - x - first]
             )
 
@@ -342,7 +387,7 @@
     copies = []
     for x, mate in ((0, DEPTH - 1), (1, DEPTH - 2)):
         for i in range(XROWS // 8):
-            enter = enter_ref[pl.ds(8 * i, 8), :]
+            enter = enter_ref[pl.ds(16 * LINE.index(i // 2) + 8 * (i % 2), 8), :]
             value = []
             for t in (x, mate):
                 at = pl.ds(t * XROWS + 8 * i, 8)
@@ -375,15 +420,16 @@
     wall = wall_mask.transpose(1, 2, 0)
 
     sources = lax.axis_size("vel")
-    shares, kept, pattern = pl.pallas_call(
+    shares, kept, pattern, weights = pl.pallas_call(
         moments_kernel,
         out_shape=[
             pltpu.VMEM((sources * SHARE, LANES), F32),
             pltpu.VMEM((DEPTH * XROWS, LANES), F32),
             pltpu.VMEM((3 + 2 * DEPTH, 8, LANES), F32),
+            pltpu.VMEM((LANES, 2 * LANES), BF16),
         ],
         in_specs=[ANYWHERE] * 4,
-        out_specs=[ON_CHIP] * 3,
+        out_specs=[ON_CHIP] * 4,
         scratch_shapes=[
             pltpu.VMEM((2, 24, LANES), F32),
             pltpu.VMEM((2, LANES), jnp.int32),
@@ -394,7 +440,12 @@
         ],
     )(f, point, mirror, wall)
     partial = lax.all_to_all(
-        shares.reshape(sources, 1, SHARE * LANES), "vel", 0, 0, tiled=True
+        shares.reshape(sources, 1, SHARE * LANES),
+        "vel",
+        0,
+        0,
+        axis_index_groups=[[*range(sources - 1, -1, -1)]],
+        tiled=True,
     ).reshape(sources * SHARE, LANES)
     cells = pl.pallas_call(
         lambda *refs: cells_kernel(sources, *refs),
@@ -411,11 +462,12 @@
             pltpu.VMEM((DEPTH * XROWS, LANES), F32),
             pltpu.VMEM((DEPTH * XROWS, LANES), F32),
         ],
-        in_specs=[ON_CHIP] * 3,
+        in_specs=[ON_CHIP] * 4,
         out_specs=[ON_CHIP] * 3,
-    )(held(everyone), held(kept), held(pattern))
+        scratch_shapes=[pltpu.VMEM((DEPTH * XROWS, 2 * LANES), F32)],
+    )(held(everyone), held(kept), held(pattern), held(weights))
     chain = lax.all_to_all(
-        send.reshape(blocks, 1, CHUNK_ROWS * LANES), "space", 0, 0, tiled=True
+        send.reshape(blocks, 1, CHUNK_ROWS * LANES), "space", 0, 0, axis_index_groups=[ORDER], tiled=True
     ).reshape(blocks * CHUNK_ROWS, LANES)
     enters = pl.pallas_call(
         lambda *refs: chain_kernel(copies, *refs),
@@ -427,7 +479,7 @@
             pltpu.VMEM((2, blocks, 8, LANES), F32),
         ],
     )(held(chain), held(pattern))
-    lines = [[CHUNKS * z + x for x in range(CHUNKS)] for z in range(copies)]
+    lines = [[CHUNKS * z + x for x in LINE] for z in range(copies)]
     enter = lax.all_to_all(enters, "space", 0, 0, axis_index_groups=lines, tiled=True)
     out = pl.pallas_call(
         finish_kernel,

time: 57.9 us -> 52.4 us (0.905)
  blocking collectives: 53 us -> 48.1 us
  Pallas kernels: 4.13 us -> 3.49 us
    all_to_all x1, blocking collectives: 23.6 us -> 20 us  [shards(): lax.all_to_all(send.reshape(blocks, 1, CHUNK_ROWS * LANES), 'space', 0, 0...]
    all_to_all x1, blocking collectives: 19.3 us -> 17.8 us  [shards(): lax.all_to_all(shares.reshape(sources, 1, SHARE * LANES), 'vel', 0, 0, ax...]
    pallas_call x1, Pallas kernels: 1.18 us -> 0.55 us  [shards(): pl.pallas_call(lambda *refs: blocks_kernel(copies, *refs), out_shape=[plt...]
where the time goes in v8:
time: 52.4 us; the launch traced here: 51.6 us
  blocking collectives  48.1 us (92%)
  Pallas kernels  3.49 us (7%)
    all_to_all x1, blocking collectives, shards(): lax.all_to_all(send.reshape(blocks, 1, CHUNK_ROWS * LANES), 'space', 0, 0...  20 us
    all_to_all x1, blocking collectives, shards(): lax.all_to_all(shares.reshape(sources, 1, SHARE * LANES), 'vel', 0, 0, ax...  17.8 us
    all_to_all x1, blocking collectives, shards(): lax.all_to_all(enters, 'space', 0, 0, axis_index_groups=lines, tiled=True)  8.4 us
    all_gather x1, blocking collectives, shards(): everyone = lax.all_gather(cells, 'vel', axis_index_groups=pairs)  1.84 us
    pallas_call x1, Pallas kernels, shards(): pl.pallas_call(moments_kernel, out_shape=[pltpu.VMEM((sources * SHARE, LA...  1.72 us

profile of v8, /device:TPU:1, one launch (start us, length us, event | category | flops | bytes accessed | tf_op | source)
XLA Modules:
  0.0 51.6 jit_solution(4063263520492183971)
XLA Ops:
  0.0 1.7 %shard_map.46 = (f32[368,128]{1,0:T(8,128)S(1)}, f32[512,128]{1,0:T(8,128)S(1)}, f32[11,8,128]{2,1,0:T(8,128)S(1)}, bf16[128,256]{1,0:T(8,128)(2,1)S(1)}) custom-call(f32[512,128]{1,0:T(8,128)} %bitcast.25, s32[2,128]{1,0:T(2,128)} %bitcast.27, s32[2,128]{1,0:T(2,128)} %bitcast.28, s32[2,2,4]{2,1,0:T(2,128)} %bitcast.26), custom_call_target="tpu_custom_call" | custom-call | tf_op jit(solution)/shard_map/pallas_call | solution.py:423
  1.7 17.8 %all_to_all.15 = f32[16,1,2944]{2,1,0:T(1,128)S(1)} all-to-all(f32[16,1,2944]{2,1,0:T(1,128)S(1)} %bitcast.23), channel_id=1, replica_groups={{15,14,13,12,11,10,9,8,7,6,5,4,3,2,1,0},{31,30,29,28,27,26,25,24,23,22,..., dimensions={0} | all-to-all | bytes 376832 | tf_op jit(solution)/shard_map/all_to_all | solution.py:442
  19.6 0.2 shard_map.47
  19.8 1.8 %all-gather = f32[10,8,128]{2,1,0:T(8,128)S(1)} all-gather(f32[5,8,128]{2,1,0:T(8,128)S(1)} %shard_map.47), channel_id=2, replica_groups={{0,1},{2,3},{4,5},{6,7},{8,9},{10,11},{12,13},{14,15},{16,17},{18,19},{..., dimensions={0}, use_global_device_ids=true | all-gather | bytes 61440 | tf_op jit(solution)/shard_map/all_gather | solution.py:457
  21.7 0.6 %shard_map.48 = (f32[544,128]{1,0:T(8,128)S(1)}, f32[512,128]{1,0:T(8,128)S(1)}, f32[512,128]{1,0:T(8,128)S(1)}) custom-call(f32[2,5,8,128]{3,2,1,0:T(8,128)S(1)} %bitcast.24, f32[512,128]{1,0:T(8,128)S(1)} %get-tuple-element.13.refs_1_, f32[11,8,128]{2,1,0:T(8,128)S(1)} %get-tuple-element.14.refs_2_.refs_1_.pattern_ref, ...), custom_call_target="tpu_custom_call" | custom-call | tf_op jit(solution)/shard_map/pallas_call | solution.py:458
  22.2 20.0 %all_to_all.16 = f32[32,1,2176]{2,1,0:T(1,128)S(1)} all-to-all(f32[32,1,2176]{2,1,0:T(1,128)S(1)} %bitcast.21), channel_id=1, replica_groups={{496,480,464,448,432,416,400,384,368,352,336,320,304,288,272,256,240,22..., dimensions={0} | all-to-all | bytes 557056 | tf_op jit(solution)/shard_map/all_to_all | solution.py:469
  42.2 0.2 shard_map.49
  42.5 8.4 %all_to_all.17 = f32[8,16,128]{2,1,0:T(8,128)S(1)} all-to-all(f32[8,16,128]{2,1,0:T(8,128)S(1)} %shard_map.49), channel_id=1, replica_groups={{112,96,80,64,48,32,16,0},{240,224,208,192,176,160,144,128},{368,352,33..., dimensions={0} | all-to-all | bytes 131072 | tf_op jit(solution)/shard_map/all_to_all | solution.py:483
  50.9 0.7 %shard_map.50 = f32[512,128]{1,0:T(8,128)} custom-call(f32[128,128]{1,0:T(8,128)S(1)} %bitcast.22, f32[512,128]{1,0:T(8,128)S(1)} %get-tuple-element.17.a_ref, f32[512,128]{1,0:T(8,128)S(1)} %get-tuple-element.18.h_ref, f32[11,8,128]{2,1,0:T(8,128)S(1)} %get-tuple-element.14.refs_2_.refs_1_.pattern_ref), custom_call_target="tpu_custom_call" | custom-call | tf_op jit(solution)/shard_map/pallas_call | solution.py:484

commit v9 on v8

--- a/solution.py
+++ b/solution.py
@@ -28,8 +28,9 @@
 CHUNKS = 8
 CHUNK_ROWS = 17
 
+VELO = [*range(11, -1, -1), *range(15, 11, -1)]
 ORDER = list(range(31, -1, -1))
-LINE = [7, 6, 5, 4, 3, 2, 1, 0]
+LINE = [6, 5, 4, 3, 2, 1, 0, 7]
 
 SHARE = 23
 
@@ -150,7 +151,7 @@
                 x2[half : half + 1] < 0, low, high
             )
         if second:
-            for to in range(1 - core, send_ref.shape[0] // SHARE, 2):
+            for to in [p for p in range(16) if VELO[p] % 2 == core]:
                 send_ref[pl.ds(SHARE * to, SHARE), :] = half_ref[core, 0:SHARE, :]
 
 
@@ -205,10 +206,10 @@
         out_ref[k] = table[8 * k : 8 * k + 8]
 
     upper = (sublane((8, LANES)) >> 2) & 1
-    even = sources - 1 - lax.axis_index("vel") // 2 * 2
+    chip = lax.axis_index("vel") // 2
     lanes, kept, rolled, values = [], [], [], []
     for core in range(2):
-        at = SHARE * (even - core) + 21
+        at = SHARE * ((11 - 2 * chip - core) % 16) + 21
         first = jnp.broadcast_to(got_ref[pl.ds(at, 1), :], (8, LANES))
         second = jnp.broadcast_to(got_ref[pl.ds(at + 1, 1), :], (8, LANES))
         slot = jnp.where(upper == 0, first, second).astype(jnp.int32)
@@ -219,7 +220,7 @@
     for k in range(sources):
         piece = got_ref[pl.ds(SHARE * k + 13, 8), :]
         swapped = pltpu.roll(piece, 4, 0)
-        owner = sources - 1 - k
+        owner = VELO[k]
         for core in range(2):
             there = jnp.take_along_axis(piece, lanes[core], axis=1)
             across = jnp.take_along_axis(swapped, lanes[core], axis=1)
@@ -444,7 +445,7 @@
         "vel",
         0,
         0,
-        axis_index_groups=[[*range(sources - 1, -1, -1)]],
+        axis_index_groups=[VELO],
         tiled=True,
     ).reshape(sources * SHARE, LANES)
     cells = pl.pallas_call(

time: 52.4 us -> 51.2 us (0.977)
  the two profiles are of different devices: /device:TPU:1 before, /device:TPU:4 now
where the time goes in v9:
time: 51.2 us; the launch traced here: 51 us
  blocking collectives  47.5 us (93%)
  Pallas kernels  3.5 us (7%)
    all_to_all x1, blocking collectives, shards(): lax.all_to_all(send.reshape(blocks, 1, CHUNK_ROWS * LANES), 'space', 0, 0...  22.7 us
    all_to_all x1, blocking collectives, shards(): lax.all_to_all(shares.reshape(sources, 1, SHARE * LANES), 'vel', 0, 0, ax...  13.9 us
    all_to_all x1, blocking collectives, shards(): lax.all_to_all(enters, 'space', 0, 0, axis_index_groups=lines, tiled=True)  9.13 us
    all_gather x1, blocking collectives, shards(): everyone = lax.all_gather(cells, 'vel', axis_index_groups=pairs)  1.84 us
    pallas_call x1, Pallas kernels, shards(): pl.pallas_call(moments_kernel, out_shape=[pltpu.VMEM((sources * SHARE, LA...  1.72 us

profile of v9, /device:TPU:4, one launch (start us, length us, event | category | flops | bytes accessed | tf_op | source)
XLA Modules:
  0.0 51.0 jit_solution(1804105108752235486)
XLA Ops:
  0.0 1.7 %shard_map.46 = (f32[368,128]{1,0:T(8,128)S(1)}, f32[512,128]{1,0:T(8,128)S(1)}, f32[11,8,128]{2,1,0:T(8,128)S(1)}, bf16[128,256]{1,0:T(8,128)(2,1)S(1)}) custom-call(f32[512,128]{1,0:T(8,128)} %bitcast.25, s32[2,128]{1,0:T(2,128)} %bitcast.27, s32[2,128]{1,0:T(2,128)} %bitcast.28, s32[2,2,4]{2,1,0:T(2,128)} %bitcast.26), custom_call_target="tpu_custom_call" | custom-call | tf_op jit(solution)/shard_map/pallas_call | solution.py:424
  1.7 13.9 %all_to_all.15 = f32[16,1,2944]{2,1,0:T(1,128)S(1)} all-to-all(f32[16,1,2944]{2,1,0:T(1,128)S(1)} %bitcast.23), channel_id=1, replica_groups={{11,10,9,8,7,6,5,4,3,2,1,0,15,14,13,12},{27,26,25,24,23,22,21,20,19,18,..., dimensions={0} | all-to-all | bytes 376832 | tf_op jit(solution)/shard_map/all_to_all | solution.py:443
  15.6 0.2 shard_map.47
  15.8 1.8 %all-gather = f32[10,8,128]{2,1,0:T(8,128)S(1)} all-gather(f32[5,8,128]{2,1,0:T(8,128)S(1)} %shard_map.47), channel_id=2, replica_groups={{0,1},{2,3},{4,5},{6,7},{8,9},{10,11},{12,13},{14,15},{16,17},{18,19},{..., dimensions={0}, use_global_device_ids=true | all-gather | bytes 61440 | tf_op jit(solution)/shard_map/all_gather | solution.py:458
  17.7 0.6 %shard_map.48 = (f32[544,128]{1,0:T(8,128)S(1)}, f32[512,128]{1,0:T(8,128)S(1)}, f32[512,128]{1,0:T(8,128)S(1)}) custom-call(f32[2,5,8,128]{3,2,1,0:T(8,128)S(1)} %bitcast.24, f32[512,128]{1,0:T(8,128)S(1)} %get-tuple-element.13.refs_1_, f32[11,8,128]{2,1,0:T(8,128)S(1)} %get-tuple-element.14.refs_2_.refs_1_.pattern_ref, ...), custom_call_target="tpu_custom_call" | custom-call | tf_op jit(solution)/shard_map/pallas_call | solution.py:459
  18.2 22.7 %all_to_all.16 = f32[32,1,2176]{2,1,0:T(1,128)S(1)} all-to-all(f32[32,1,2176]{2,1,0:T(1,128)S(1)} %bitcast.21), channel_id=1, replica_groups={{496,480,464,448,432,416,400,384,368,352,336,320,304,288,272,256,240,22..., dimensions={0} | all-to-all | bytes 557056 | tf_op jit(solution)/shard_map/all_to_all | solution.py:470
  40.9 0.2 shard_map.49
  41.1 9.1 %all_to_all.17 = f32[8,16,128]{2,1,0:T(8,128)S(1)} all-to-all(f32[8,16,128]{2,1,0:T(8,128)S(1)} %shard_map.49), channel_id=1, replica_groups={{96,80,64,48,32,16,0,112},{224,208,192,176,160,144,128,240},{352,336,32..., dimensions={0} | all-to-all | bytes 131072 | tf_op jit(solution)/shard_map/all_to_all | solution.py:484
  50.3 0.8 %shard_map.50 = f32[512,128]{1,0:T(8,128)} custom-call(f32[128,128]{1,0:T(8,128)S(1)} %bitcast.22, f32[512,128]{1,0:T(8,128)S(1)} %get-tuple-element.17.a_ref, f32[512,128]{1,0:T(8,128)S(1)} %get-tuple-element.18.h_ref, f32[11,8,128]{2,1,0:T(8,128)S(1)} %get-tuple-element.14.refs_2_.refs_1_.pattern_ref), custom_call_target="tpu_custom_call" | custom-call | tf_op jit(solution)/shard_map/pallas_call | solution.py:485

commit v10 on v9

--- a/solution.py
+++ b/solution.py
@@ -28,7 +28,7 @@
 CHUNKS = 8
 CHUNK_ROWS = 17
 
-VELO = [*range(11, -1, -1), *range(15, 11, -1)]
+VELO = [*range(9, -1, -1), *range(15, 9, -1)]
 ORDER = list(range(31, -1, -1))
 LINE = [6, 5, 4, 3, 2, 1, 0, 7]
 
@@ -209,7 +209,7 @@
     chip = lax.axis_index("vel") // 2
     lanes, kept, rolled, values = [], [], [], []
     for core in range(2):
-        at = SHARE * ((11 - 2 * chip - core) % 16) + 21
+        at = SHARE * ((9 - 2 * chip - core) % 16) + 21
         first = jnp.broadcast_to(got_ref[pl.ds(at, 1), :], (8, LANES))
         second = jnp.broadcast_to(got_ref[pl.ds(at + 1, 1), :], (8, LANES))
         slot = jnp.where(upper == 0, first, second).astype(jnp.int32)

time: 51.2 us -> 50.8 us (level)
  no operation moved by 1% of the time
where the time goes in v10:
time: 50.8 us; the launch traced here: 50.6 us
  blocking collectives  47.1 us (93%)
  Pallas kernels  3.5 us (7%)
    all_to_all x1, blocking collectives, shards(): lax.all_to_all(send.reshape(blocks, 1, CHUNK_ROWS * LANES), 'space', 0, 0...  22.7 us
    all_to_all x1, blocking collectives, shards(): lax.all_to_all(shares.reshape(sources, 1, SHARE * LANES), 'vel', 0, 0, ax...  13.5 us
    all_to_all x1, blocking collectives, shards(): lax.all_to_all(enters, 'space', 0, 0, axis_index_groups=lines, tiled=True)  9.13 us
    all_gather x1, blocking collectives, shards(): everyone = lax.all_gather(cells, 'vel', axis_index_groups=pairs)  1.84 us
    pallas_call x1, Pallas kernels, shards(): pl.pallas_call(moments_kernel, out_shape=[pltpu.VMEM((sources * SHARE, LA...  1.72 us

profile of v10, /device:TPU:4, one launch (start us, length us, event | category | flops | bytes accessed | tf_op | source)
XLA Modules:
  0.0 50.6 jit_solution(2244188953873409647)
XLA Ops:
  0.0 1.7 %shard_map.46 = (f32[368,128]{1,0:T(8,128)S(1)}, f32[512,128]{1,0:T(8,128)S(1)}, f32[11,8,128]{2,1,0:T(8,128)S(1)}, bf16[128,256]{1,0:T(8,128)(2,1)S(1)}) custom-call(f32[512,128]{1,0:T(8,128)} %bitcast.25, s32[2,128]{1,0:T(2,128)} %bitcast.27, s32[2,128]{1,0:T(2,128)} %bitcast.28, s32[2,2,4]{2,1,0:T(2,128)} %bitcast.26), custom_call_target="tpu_custom_call" | custom-call | tf_op jit(solution)/shard_map/pallas_call | solution.py:424
  1.7 13.5 %all_to_all.15 = f32[16,1,2944]{2,1,0:T(1,128)S(1)} all-to-all(f32[16,1,2944]{2,1,0:T(1,128)S(1)} %bitcast.23), channel_id=1, replica_groups={{9,8,7,6,5,4,3,2,1,0,15,14,13,12,11,10},{25,24,23,22,21,20,19,18,17,16,..., dimensions={0} | all-to-all | bytes 376832 | tf_op jit(solution)/shard_map/all_to_all | solution.py:443
  15.2 0.2 shard_map.47
  15.4 1.8 %all-gather = f32[10,8,128]{2,1,0:T(8,128)S(1)} all-gather(f32[5,8,128]{2,1,0:T(8,128)S(1)} %shard_map.47), channel_id=2, replica_groups={{0,1},{2,3},{4,5},{6,7},{8,9},{10,11},{12,13},{14,15},{16,17},{18,19},{..., dimensions={0}, use_global_device_ids=true | all-gather | bytes 61440 | tf_op jit(solution)/shard_map/all_gather | solution.py:458
  17.3 0.6 %shard_map.48 = (f32[544,128]{1,0:T(8,128)S(1)}, f32[512,128]{1,0:T(8,128)S(1)}, f32[512,128]{1,0:T(8,128)S(1)}) custom-call(f32[2,5,8,128]{3,2,1,0:T(8,128)S(1)} %bitcast.24, f32[512,128]{1,0:T(8,128)S(1)} %get-tuple-element.13.refs_1_, f32[11,8,128]{2,1,0:T(8,128)S(1)} %get-tuple-element.14.refs_2_.refs_1_.pattern_ref, ...), custom_call_target="tpu_custom_call" | custom-call | tf_op jit(solution)/shard_map/pallas_call | solution.py:459
  17.8 22.7 %all_to_all.16 = f32[32,1,2176]{2,1,0:T(1,128)S(1)} all-to-all(f32[32,1,2176]{2,1,0:T(1,128)S(1)} %bitcast.21), channel_id=1, replica_groups={{496,480,464,448,432,416,400,384,368,352,336,320,304,288,272,256,240,22..., dimensions={0} | all-to-all | bytes 557056 | tf_op jit(solution)/shard_map/all_to_all | solution.py:470
  40.5 0.2 shard_map.49
  40.7 9.1 %all_to_all.17 = f32[8,16,128]{2,1,0:T(8,128)S(1)} all-to-all(f32[8,16,128]{2,1,0:T(8,128)S(1)} %shard_map.49), channel_id=1, replica_groups={{96,80,64,48,32,16,0,112},{224,208,192,176,160,144,128,240},{352,336,32..., dimensions={0} | all-to-all | bytes 131072 | tf_op jit(solution)/shard_map/all_to_all | solution.py:484
  49.9 0.8 %shard_map.50 = f32[512,128]{1,0:T(8,128)} custom-call(f32[128,128]{1,0:T(8,128)S(1)} %bitcast.22, f32[512,128]{1,0:T(8,128)S(1)} %get-tuple-element.17.a_ref, f32[512,128]{1,0:T(8,128)S(1)} %get-tuple-element.18.h_ref, f32[11,8,128]{2,1,0:T(8,128)S(1)} %get-tuple-element.14.refs_2_.refs_1_.pattern_ref), custom_call_target="tpu_custom_call" | custom-call | tf_op jit(solution)/shard_map/pallas_call | solution.py:485

commit v11 on v10

--- a/solution.py
+++ b/solution.py
@@ -29,8 +29,8 @@
 CHUNK_ROWS = 17
 
 VELO = [*range(9, -1, -1), *range(15, 9, -1)]
-ORDER = list(range(31, -1, -1))
 LINE = [6, 5, 4, 3, 2, 1, 0, 7]
+ORDER = [8 * z + x for z in range(3, -1, -1) for x in LINE]
 
 SHARE = 23
 

time: 50.8 us -> 50.9 us (level)
  the two profiles are of different devices: /device:TPU:4 before, /device:TPU:1 now
where the time goes in v11:
time: 50.9 us; the launch traced here: 49.9 us
  blocking collectives  46.4 us (91%)
  Pallas kernels  3.5 us (7%)
    all_to_all x1, blocking collectives, shards(): lax.all_to_all(shares.reshape(sources, 1, SHARE * LANES), 'vel', 0, 0, ax...  18.7 us
    all_to_all x1, blocking collectives, shards(): lax.all_to_all(send.reshape(blocks, 1, CHUNK_ROWS * LANES), 'space', 0, 0...  16.9 us
    all_to_all x1, blocking collectives, shards(): lax.all_to_all(enters, 'space', 0, 0, axis_index_groups=lines, tiled=True)  8.63 us
    all_gather x1, blocking collectives, shards(): everyone = lax.all_gather(cells, 'vel', axis_index_groups=pairs)  2.11 us
    pallas_call x1, Pallas kernels, shards(): pl.pallas_call(moments_kernel, out_shape=[pltpu.VMEM((sources * SHARE, LA...  1.72 us

profile of v11, /device:TPU:1, one launch (start us, length us, event | category | flops | bytes accessed | tf_op | source)
XLA Modules:
  0.0 49.9 jit_solution(6438543424381730497)
XLA Ops:
  0.0 1.7 %shard_map.46 = (f32[368,128]{1,0:T(8,128)S(1)}, f32[512,128]{1,0:T(8,128)S(1)}, f32[11,8,128]{2,1,0:T(8,128)S(1)}, bf16[128,256]{1,0:T(8,128)(2,1)S(1)}) custom-call(f32[512,128]{1,0:T(8,128)} %bitcast.25, s32[2,128]{1,0:T(2,128)} %bitcast.27, s32[2,128]{1,0:T(2,128)} %bitcast.28, s32[2,2,4]{2,1,0:T(2,128)} %bitcast.26), custom_call_target="tpu_custom_call" | custom-call | tf_op jit(solution)/shard_map/pallas_call | solution.py:424
  1.7 18.7 %all_to_all.15 = f32[16,1,2944]{2,1,0:T(1,128)S(1)} all-to-all(f32[16,1,2944]{2,1,0:T(1,128)S(1)} %bitcast.23), channel_id=1, replica_groups={{9,8,7,6,5,4,3,2,1,0,15,14,13,12,11,10},{25,24,23,22,21,20,19,18,17,16,..., dimensions={0} | all-to-all | bytes 376832 | tf_op jit(solution)/shard_map/all_to_all | solution.py:443
  20.5 0.2 shard_map.47
  20.7 2.1 %all-gather = f32[10,8,128]{2,1,0:T(8,128)S(1)} all-gather(f32[5,8,128]{2,1,0:T(8,128)S(1)} %shard_map.47), channel_id=2, replica_groups={{0,1},{2,3},{4,5},{6,7},{8,9},{10,11},{12,13},{14,15},{16,17},{18,19},{..., dimensions={0}, use_global_device_ids=true | all-gather | bytes 61440 | tf_op jit(solution)/shard_map/all_gather | solution.py:458
  22.8 0.6 %shard_map.48 = (f32[544,128]{1,0:T(8,128)S(1)}, f32[512,128]{1,0:T(8,128)S(1)}, f32[512,128]{1,0:T(8,128)S(1)}) custom-call(f32[2,5,8,128]{3,2,1,0:T(8,128)S(1)} %bitcast.24, f32[512,128]{1,0:T(8,128)S(1)} %get-tuple-element.13.refs_1_, f32[11,8,128]{2,1,0:T(8,128)S(1)} %get-tuple-element.14.refs_2_.refs_1_.pattern_ref, ...), custom_call_target="tpu_custom_call" | custom-call | tf_op jit(solution)/shard_map/pallas_call | solution.py:459
  23.4 16.9 %all_to_all.16 = f32[32,1,2176]{2,1,0:T(1,128)S(1)} all-to-all(f32[32,1,2176]{2,1,0:T(1,128)S(1)} %bitcast.21), channel_id=1, replica_groups={{480,464,448,432,416,400,384,496,352,336,320,304,288,272,256,368,224,20..., dimensions={0} | all-to-all | bytes 557056 | tf_op jit(solution)/shard_map/all_to_all | solution.py:470
  40.3 0.2 shard_map.49
  40.6 8.6 %all_to_all.17 = f32[8,16,128]{2,1,0:T(8,128)S(1)} all-to-all(f32[8,16,128]{2,1,0:T(8,128)S(1)} %shard_map.49), channel_id=1, replica_groups={{96,80,64,48,32,16,0,112},{224,208,192,176,160,144,128,240},{352,336,32..., dimensions={0} | all-to-all | bytes 131072 | tf_op jit(solution)/shard_map/all_to_all | solution.py:484
  49.2 0.8 %shard_map.50 = f32[512,128]{1,0:T(8,128)} custom-call(f32[128,128]{1,0:T(8,128)S(1)} %bitcast.22, f32[512,128]{1,0:T(8,128)S(1)} %get-tuple-element.17.a_ref, f32[512,128]{1,0:T(8,128)S(1)} %get-tuple-element.18.h_ref, f32[11,8,128]{2,1,0:T(8,128)S(1)} %get-tuple-element.14.refs_2_.refs_1_.pattern_ref), custom_call_target="tpu_custom_call" | custom-call | tf_op jit(solution)/shard_map/pallas_call | solution.py:485

commit v12 on v11

--- a/solution.py
+++ b/solution.py
@@ -28,7 +28,7 @@
 CHUNKS = 8
 CHUNK_ROWS = 17
 
-VELO = [*range(9, -1, -1), *range(15, 9, -1)]
+VELO = [8, 9, 6, 7, 4, 5, 2, 3, 0, 1, 14, 15, 12, 13, 10, 11]
 LINE = [6, 5, 4, 3, 2, 1, 0, 7]
 ORDER = [8 * z + x for z in range(3, -1, -1) for x in LINE]
 
@@ -209,7 +209,7 @@
     chip = lax.axis_index("vel") // 2
     lanes, kept, rolled, values = [], [], [], []
     for core in range(2):
-        at = SHARE * ((9 - 2 * chip - core) % 16) + 21
+        at = SHARE * ((8 - 2 * chip) % 16 + core) + 21
         first = jnp.broadcast_to(got_ref[pl.ds(at, 1), :], (8, LANES))
         second = jnp.broadcast_to(got_ref[pl.ds(at + 1, 1), :], (8, LANES))
         slot = jnp.where(upper == 0, first, second).astype(jnp.int32)

time: 50.9 us -> 51.5 us (1.012)
  blocking collectives: 46.4 us -> 47 us
where the time goes in v12:
time: 51.5 us; the launch traced here: 50.5 us
  blocking collectives  47 us (91%)
  Pallas kernels  3.5 us (7%)
    all_to_all x1, blocking collectives, shards(): lax.all_to_all(shares.reshape(sources, 1, SHARE * LANES), 'vel', 0, 0, ax...  18.8 us
    all_to_all x1, blocking collectives, shards(): lax.all_to_all(send.reshape(blocks, 1, CHUNK_ROWS * LANES), 'space', 0, 0...  17.2 us
    all_to_all x1, blocking collectives, shards(): lax.all_to_all(enters, 'space', 0, 0, axis_index_groups=lines, tiled=True)  8.63 us
    all_gather x1, blocking collectives, shards(): everyone = lax.all_gather(cells, 'vel', axis_index_groups=pairs)  2.28 us
    pallas_call x1, Pallas kernels, shards(): pl.pallas_call(moments_kernel, out_shape=[pltpu.VMEM((sources * SHARE, LA...  1.72 us

profile of v12, /device:TPU:1, one launch (start us, length us, event | category | flops | bytes accessed | tf_op | source)
XLA Modules:
  0.0 50.5 jit_solution(340751992179947573)
XLA Ops:
  0.0 1.7 %shard_map.46 = (f32[368,128]{1,0:T(8,128)S(1)}, f32[512,128]{1,0:T(8,128)S(1)}, f32[11,8,128]{2,1,0:T(8,128)S(1)}, bf16[128,256]{1,0:T(8,128)(2,1)S(1)}) custom-call(f32[512,128]{1,0:T(8,128)} %bitcast.25, s32[2,128]{1,0:T(2,128)} %bitcast.27, s32[2,128]{1,0:T(2,128)} %bitcast.28, s32[2,2,4]{2,1,0:T(2,128)} %bitcast.26), custom_call_target="tpu_custom_call" | custom-call | tf_op jit(solution)/shard_map/pallas_call | solution.py:424
  1.7 18.8 %all_to_all.15 = f32[16,1,2944]{2,1,0:T(1,128)S(1)} all-to-all(f32[16,1,2944]{2,1,0:T(1,128)S(1)} %bitcast.23), channel_id=1, replica_groups={{8,9,6,7,4,5,2,3,0,1,14,15,12,13,10,11},{24,25,22,23,20,21,18,19,16,17,..., dimensions={0} | all-to-all | bytes 376832 | tf_op jit(solution)/shard_map/all_to_all | solution.py:443
  20.6 0.2 shard_map.47
  20.8 2.3 %all-gather = f32[10,8,128]{2,1,0:T(8,128)S(1)} all-gather(f32[5,8,128]{2,1,0:T(8,128)S(1)} %shard_map.47), channel_id=2, replica_groups={{0,1},{2,3},{4,5},{6,7},{8,9},{10,11},{12,13},{14,15},{16,17},{18,19},{..., dimensions={0}, use_global_device_ids=true | all-gather | bytes 61440 | tf_op jit(solution)/shard_map/all_gather | solution.py:458
  23.1 0.6 %shard_map.48 = (f32[544,128]{1,0:T(8,128)S(1)}, f32[512,128]{1,0:T(8,128)S(1)}, f32[512,128]{1,0:T(8,128)S(1)}) custom-call(f32[2,5,8,128]{3,2,1,0:T(8,128)S(1)} %bitcast.24, f32[512,128]{1,0:T(8,128)S(1)} %get-tuple-element.13.refs_1_, f32[11,8,128]{2,1,0:T(8,128)S(1)} %get-tuple-element.14.refs_2_.refs_1_.pattern_ref, ...), custom_call_target="tpu_custom_call" | custom-call | tf_op jit(solution)/shard_map/pallas_call | solution.py:459
  23.6 17.2 %all_to_all.16 = f32[32,1,2176]{2,1,0:T(1,128)S(1)} all-to-all(f32[32,1,2176]{2,1,0:T(1,128)S(1)} %bitcast.21), channel_id=1, replica_groups={{480,464,448,432,416,400,384,496,352,336,320,304,288,272,256,368,224,20..., dimensions={0} | all-to-all | bytes 557056 | tf_op jit(solution)/shard_map/all_to_all | solution.py:470
  40.9 0.2 shard_map.49
  41.1 8.6 %all_to_all.17 = f32[8,16,128]{2,1,0:T(8,128)S(1)} all-to-all(f32[8,16,128]{2,1,0:T(8,128)S(1)} %shard_map.49), channel_id=1, replica_groups={{96,80,64,48,32,16,0,112},{224,208,192,176,160,144,128,240},{352,336,32..., dimensions={0} | all-to-all | bytes 131072 | tf_op jit(solution)/shard_map/all_to_all | solution.py:484
  49.8 0.8 %shard_map.50 = f32[512,128]{1,0:T(8,128)} custom-call(f32[128,128]{1,0:T(8,128)S(1)} %bitcast.22, f32[512,128]{1,0:T(8,128)S(1)} %get-tuple-element.17.a_ref, f32[512,128]{1,0:T(8,128)S(1)} %get-tuple-element.18.h_ref, f32[11,8,128]{2,1,0:T(8,128)S(1)} %get-tuple-element.14.refs_2_.refs_1_.pattern_ref), custom_call_target="tpu_custom_call" | custom-call | tf_op jit(solution)/shard_map/pallas_call | solution.py:485
